TPU v7x, 32 devices: a whole 2x2x4 slice. The times are simulated.
32 devices in a mesh: airway: 4 (over y, core), section: 8 (over z, x).
Axes of the slice: x: 2, y: 2, z: 4, core: 2. Of those that a mesh axis runs over, the one named last changes fastest.
Arguments:
- fluid_velocity: float32 [3, 64, 64, 1024], P(None, None, 'section', 'airway'), may hold values from -6 to 6
- viscosity: float32 [64, 1024], P('section', 'airway'), may hold values from 0.002 to 0.008
- axial_speed: float32 [64, 1024], P('section', 'airway'), may hold values from 0.01 to 0.04
- fluid_mass: float32 [64, 1024], P('section', 'airway'), may hold values from 2 to 8
- positions: float32 [3072, 3, 128], P(('airway', 'section')), may hold values from -1 to 1
- velocities: float32 [3072, 3, 128], P(('airway', 'section')), may hold values from -6 to 6
- relax_rates: float32 [3072, 128], P(('airway', 'section')), may hold values from 0.02 to 0.5
- bin_element: int32 [3072], P(('airway', 'section')), may hold values from 0 to 2047
- bin_fill: int32 [3072], P(('airway', 'section')), may hold values from 0 to 128, as said below
Outputs:
- fluid_out: float32 [3, 64, 64, 1024], P(None, None, 'section', 'airway')
- particles_out: float32 [3072, 6, 128], P(('airway', 'section'))
Inputs may be any that keep to these rules, and one draw needn't show every extreme that they name: `bin_fill`: on each device the bins with particles are the first 64 + k slots, k from 0 to 32; over all devices the k sum to exactly 512, and k = 32 on some device. Every device's first slot holds 128 particles.
All inputs are finite; a program needn't handle non-finite values.
Results may differ from a plain program's by a relative error of at most 0.00023.
Values sent between devices are 32-bit elements; how exact they have to be, the bound alone decides.
No kernel may reach another device: no remote copies, remote signals or barrier semaphores. Data moves between devices by JAX's collectives and lax.ppermute only.
A program may use at most 64 MiB of HBM per device.

v0:
```python
import functools

import jax
import jax.numpy as jnp
import numpy as np
from jax import lax
from jax.experimental import pallas as pl
from jax.experimental.pallas import tpu as pltpu
from jax.sharding import PartitionSpec as P

NODES = 64
SUBSTEPS = 16
PASSES = 4
SUB = 8
LANE = 128
GROUPS_TOGETHER = 4

penalty_weight = 0.25
stride_step = 0.05
f32 = jnp.float32
bf16 = jnp.bfloat16


def iota(shape, dim):
    return lax.broadcasted_iota(jnp.int32, shape, dim)


def split(value):
    high = value.astype(bf16)
    low = (value - high.astype(f32)).astype(bf16)
    return high, low


def dot(a, b):
    return lax.dot_general(a, b, (((1,), (0,)), ((), ())), preferred_element_type=f32)


def dot_t(a, b):
    return lax.dot_general(a, b, (((1,), (1,)), ((), ())), preferred_element_type=f32)


def basis_values(x):
    square = x * x
    outer = 0.5625 * square - 0.0625
    inner = 1.6875 - 1.6875 * square
    outer_x = outer * x
    inner_x = inner * x
    third = inner * (1.0 / 3.0)
    return [outer - outer_x, third - inner_x, third + inner_x, outer + outer_x]


def send_faces(q, sa_next, sa_prev, ss_next, ss_prev):
    cells = q.shape[-1]
    lane = iota((SUB, LANE), 1)
    nxt = jnp.zeros((SUB, LANE), f32)
    prv = jnp.zeros((SUB, LANE), f32)
    for comp in range(3):
        for b in range(4):
            for c in range(4):
                i = comp * 16 + b * 4 + c
                tail = q[comp, 3, b, c, :, cells - LANE :]
                head = q[comp, 0, b, c, :, :LANE]
                nxt = jnp.where(lane == i, pltpu.roll(tail, (i + 1) % LANE, 1), nxt)
                prv = jnp.where(lane == i, pltpu.roll(head, i, 1), prv)
    sa_next[...] = nxt
    sa_prev[...] = prv
    for comp in range(3):
        for a in range(4):
            for c in range(4):
                i = a * 4 + c
                ss_next[comp, i : i + 1, :] = q[comp, a, 3, c, SUB - 1 : SUB, :]
                ss_prev[comp, i : i + 1, :] = q[comp, a, 0, c, 0:1, :]


def second_line(q, v_even, v_odd):
    even = v_even * ((q[0] + q[3]) - (q[1] + q[2]))
    odd = v_odd * ((q[3] - q[0]) - 3.0 * (q[2] - q[1]))
    third = odd * (1.0 / 3.0)
    return [even - odd, even - third, even + third, even + odd]


def pass_kernel(last, q, visc, speed, ha_after, ha_before, hs_after, hs_before, out, *sends):
    cells = q.shape[-1]
    tiles = cells // LANE
    lane = iota((SUB, LANE), 1)
    row = iota((SUB, LANE), 0)
    is_last_lane = lane == LANE - 1
    is_first_lane = lane == 0
    is_last_row = row == SUB - 1
    is_first_row = row == 0

    def component(comp, carry):
        halo_after = ha_after[...]
        halo_before = ha_before[...]
        for j in range(tiles):
            at = pl.ds(j * LANE, LANE)
            v_even = visc[:, at] * 1.125
            v_odd = visc[:, at] * 3.375
            s_even = speed[:, at] * 1.125
            s_odd = speed[:, at] * 1.125
            s_half = speed[:, at] * 0.5
            for b in range(4):
                plane = [[q[comp, a, b, c, :, at] for c in range(4)] for a in range(4)]
                along_c = [second_line(plane[a], v_even, v_odd) for a in range(4)]
                for c in range(4):
                    line = [plane[a][c] for a in range(4)]
                    rise = line[3] - line[0]
                    even = (line[0] + line[3]) - (line[1] + line[2])
                    odd = rise - 3.0 * (line[2] - line[1])
                    l_even = v_even * even
                    l_odd = v_odd * odd
                    l_third = l_odd * (1.0 / 3.0)
                    g_even = s_even * even
                    g_odd = s_odd * odd
                    g_rise = s_half * rise
                    g_even3 = g_even * (1.0 / 3.0)
                    g_outer = g_rise + g_odd
                    g_inner = g_rise - g_odd * (1.0 / 3.0)
                    new = [
                        (l_even + g_even) - (l_odd + g_outer),
                        (l_even + g_even3) - (l_third + g_inner),
                        (l_even - g_even3) + (l_third - g_inner),
                        (l_even - g_even) + (l_odd - g_outer),
                    ]
                    new = [line[a] + (new[a] + along_c[a][c]) for a in range(4)]
                    here = pltpu.roll(line[0], LANE - 1, 1)
                    if j == tiles - 1:
                        beyond = pltpu.roll(halo_after, (LANE - 1 - (comp * 16 + b * 4 + c)) % LANE, 1)
                    else:
                        beyond = pltpu.roll(q[comp, 0, b, c, :, pl.ds((j + 1) * LANE, LANE)], LANE - 1, 1)
                    after = jnp.where(is_last_lane, beyond, here)
                    here = pltpu.roll(line[3], 1, 1)
                    if j == 0:
                        beyond = pltpu.roll(halo_before, (LANE - (comp * 16 + b * 4 + c)) % LANE, 1)
                    else:
                        beyond = pltpu.roll(q[comp, 3, b, c, :, pl.ds((j - 1) * LANE, LANE)], 1, 1)
                    before = jnp.where(is_first_lane, beyond, here)
                    new[3] = new[3] + penalty_weight * (after - line[3])
                    new[0] = new[0] + penalty_weight * (before - line[0])
                    for a in range(4):
                        out[comp, a, b, c, :, at] = new[a]
            for a in range(4):
                for c in range(4):
                    line = [q[comp, a, b, c, :, at] for b in range(4)]
                    new = second_line(line, v_even, v_odd)
                    after = jnp.where(
                        is_last_row,
                        jnp.broadcast_to(hs_after[comp, a * 4 + c : a * 4 + c + 1, at], (SUB, LANE)),
                        pltpu.roll(line[0], SUB - 1, 0),
                    )
                    before = jnp.where(
                        is_first_row,
                        jnp.broadcast_to(hs_before[comp, a * 4 + c : a * 4 + c + 1, at], (SUB, LANE)),
                        pltpu.roll(line[3], 1, 0),
                    )
                    new[3] = new[3] + penalty_weight * (after - line[3])
                    new[0] = new[0] + penalty_weight * (before - line[0])
                    for b in range(4):
                        out[comp, a, b, c, :, at] = out[comp, a, b, c, :, at] + new[b]
        return carry

    lax.fori_loop(0, 3, component, 0)
    if not last:
        send_faces(out, *sends)


def particle_kernel(
    fluid,
    mass,
    positions,
    velocities,
    relax,
    element_row,
    fill_row,
    q_out,
    parts_out,
    sa_next,
    sa_prev,
    ss_next,
    ss_prev,
    state,
    rates,
    strides,
    occupied,
    nodal,
    sums,
    one_hot,
    rows_ref,
):
    bins = positions.shape[0]
    groups = bins // SUB
    lanes_bins = one_hot.shape[0]
    cells = fluid.shape[-1]
    row8 = iota((SUB, LANE), 0)
    lane8 = iota((SUB, LANE), 1)
    same = (lane8 % SUB == row8).astype(f32)

    rows_ref[...] = jnp.full(rows_ref.shape, -1.0, f32)
    rows_ref[0:1, :bins] = element_row[...].astype(f32)
    rows_ref[1:2, :bins] = fill_row[...].astype(f32)
    element_lanes = rows_ref[0:1, :]
    section_lanes = jnp.zeros_like(element_lanes)
    for s in range(1, SUB):
        section_lanes = section_lanes + (element_lanes >= float(s * cells)).astype(f32)

    lane_bins = iota((SUB, lanes_bins), 1)
    row_bins = iota((SUB, lanes_bins), 0)
    one_hot[...] = jnp.zeros(one_hot.shape, bf16)
    section_cols = []
    for g in range(groups):
        own = lane_bins == row_bins + g * SUB
        element = jnp.sum(jnp.where(own, element_lanes, 0.0), axis=1, keepdims=True)
        fill = jnp.sum(jnp.where(own, rows_ref[1:2, :], 0.0), axis=1, keepdims=True)
        section = jnp.zeros_like(element)
        for s in range(1, SUB):
            section = section + (element >= float(s * cells)).astype(f32)
        section_cols.append(section)
        column = element - section * float(cells)
        at = pl.ds(g * SUB, SUB)
        occ = (lane8.astype(f32) < fill).astype(f32)
        occupied[at, :] = occ
        rates[at, :] = relax[at, :] * occ
        strides[at, :] = occ * stride_step
        for k in range(3):
            state[k, at, :] = positions[at, k, :]
            state[3 + k, at, :] = velocities[at, k, :]
        hot = (iota((SUB, cells), 1).astype(f32) == column).astype(f32)
        one_hot[at, :] = hot.astype(bf16)

    spread = (iota((LANE, LANE), 0) // SUB == iota((LANE, LANE), 1) // SUB).astype(bf16)
    section_col = jnp.concatenate(section_cols, axis=0)
    in_section = (iota((bins, LANE), 1) % SUB).astype(f32) == section_col
    hot_bins = one_hot[:bins, :]
    for comp in range(3):
        for a in range(4):
            i = comp * 4 + a
            values = fluid[comp, a].reshape(16 * SUB, cells)
            for part, source in enumerate(split(values)):
                picked = jnp.where(in_section, dot_t(hot_bins, source), 0.0).astype(bf16)
                wide = dot(picked, spread)
                for g in range(groups):
                    block = (wide[g * SUB : (g + 1) * SUB, :] * same).astype(f32)
                    nodal[g, part, i * SUB : (i + 1) * SUB, :] = block.astype(bf16)

    sums[...] = jnp.zeros(sums.shape, f32)

    def substep(first, turn, carry):
        for g in range(first, first + GROUPS_TOGETHER):
            at = pl.ds(g * SUB, SUB)
            x = [state[k, at, :] for k in range(3)]
            v = [state[3 + k, at, :] for k in range(3)]
            rate = rates[at, :]
            step = strides[at, :]
            occ = occupied[at, :]
            la, lb, lc = [basis_values(x[k]) for k in range(3)]
            across = jnp.concatenate([lb[b] * lc[c] for b in range(4) for c in range(4)], axis=0)
            high, low = split(across)
            n_high = nodal[g, 0]
            n_low = nodal[g, 1]
            at_a = dot(n_high, high) + (dot(n_high, low) + dot(n_low, high))
            pushes = []
            for k in range(3):
                rows = [at_a[(k * 4 + a) * SUB : (k * 4 + a + 1) * SUB, :] for a in range(4)]
                u = (la[0] * rows[0] + la[1] * rows[1]) + (la[2] * rows[2] + la[3] * rows[3])
                dv = rate * (u - v[k])
                moved = v[k] + dv
                state[3 + k, at, :] = moved
                state[k, at, :] = jnp.clip(x[k] + step * moved, -1.0, 1.0)
                pushes += [la[a] * dv for a in range(4)]
            push_high, push_low = split(jnp.concatenate(pushes, axis=0))
            drag = dot_t(push_high, high) + (dot_t(push_high, low) + dot_t(push_low, high))
            square_high, square_low = split(across * across)
            weigh_high, weigh_low = split(
                jnp.concatenate([la[a] * la[a] * occ for a in range(4)], axis=0)
            )
            weight = dot_t(weigh_high, square_high) + (
                dot_t(weigh_high, square_low) + dot_t(weigh_low, square_high)
            )
            sums[g] = sums[g] + jnp.concatenate([drag, weight], axis=0)
        return carry

    for first in range(0, groups, GROUPS_TOGETHER):
        lax.fori_loop(0, SUBSTEPS, functools.partial(substep, first), 0)

    for g in range(groups):
        at = pl.ds(g * SUB, SUB)
        for k in range(6):
            parts_out[at, k, :] = state[k, at, :]

    in_section_rows = (iota((LANE, lanes_bins), 0) % SUB).astype(f32) == section_lanes
    hot_all = one_hot[...]
    spread2 = spread

    def deposit(i):
        blocks = [sums[g, i * SUB : (i + 1) * SUB, :] * same for g in range(groups)]
        blocks += [jnp.zeros((SUB, LANE), f32)] * (lanes_bins // SUB - groups)
        high, low = split(jnp.concatenate(blocks, axis=0))
        wide = dot_t(spread2, high) + dot_t(spread2, low)
        wide = jnp.where(in_section_rows, wide, 0.0)
        high, low = split(wide)
        return dot(high, hot_all) + dot(low, hot_all)

    for a in range(4):
        weight = deposit(12 + a).reshape(4, 4, SUB, cells)
        scale = 1.0 / (mass[...][None, None] + weight)
        for comp in range(3):
            drag = deposit(comp * 4 + a).reshape(4, 4, SUB, cells)
            q_out[comp, a] = fluid[comp, a] - drag * scale

    send_faces(q_out, sa_next, sa_prev, ss_next, ss_prev)


def shift(values, axis, up):
    count = lax.axis_size(axis)
    ends = count - 1
    if up:
        pairs = [(i, i + 1) for i in range(ends)]
    else:
        pairs = [(i + 1, i) for i in range(ends)]
    return lax.ppermute(values, axis, pairs)


def exchange(faces):
    sa_next, sa_prev, ss_next, ss_prev = faces
    ha_before = shift(sa_next, "airway", True)
    ha_after = shift(sa_prev, "airway", False)
    hs_before = shift(ss_next, "section", True)
    hs_after = shift(ss_prev, "section", False)
    return ha_after, ha_before, hs_after, hs_before


def local(
    fluid_velocity,
    viscosity,
    axial_speed,
    fluid_mass,
    positions,
    velocities,
    relax_rates,
    bin_element,
    bin_fill,
):
    sec_cells, air_cells = fluid_velocity.shape[2:]
    bins = positions.shape[0]
    groups = bins // SUB
    lanes_bins = -(-bins // LANE) * LANE
    field_shape = (3, 4, 4, 4, sec_cells, air_cells)
    field = jax.ShapeDtypeStruct(field_shape, f32)
    face_shapes = (
        jax.ShapeDtypeStruct((sec_cells, LANE), f32),
        jax.ShapeDtypeStruct((sec_cells, LANE), f32),
        jax.ShapeDtypeStruct((3, 16, air_cells), f32),
        jax.ShapeDtypeStruct((3, 16, air_cells), f32),
    )
    vmem = pl.BlockSpec(memory_space=pltpu.VMEM)
    params = pltpu.CompilerParams(vmem_limit_bytes=48 * 1024 * 1024)
    q, particles_out, *faces = pl.pallas_call(
        particle_kernel,
        out_shape=(field, jax.ShapeDtypeStruct((bins, 6, LANE), f32)) + face_shapes,
        in_specs=[vmem] * 7,
        out_specs=(vmem,) * 6,
        scratch_shapes=[
            pltpu.VMEM((6, bins, LANE), f32),
            pltpu.VMEM((bins, LANE), f32),
            pltpu.VMEM((bins, LANE), f32),
            pltpu.VMEM((bins, LANE), f32),
            pltpu.VMEM((groups, 2, 96, LANE), bf16),
            pltpu.VMEM((groups, LANE, LANE), f32),
            pltpu.VMEM((lanes_bins, air_cells), bf16),
            pltpu.VMEM((SUB, lanes_bins), f32),
        ],
        compiler_params=params,
        name="particles",
    )(
        fluid_velocity.reshape(field_shape),
        fluid_mass,
        positions,
        velocities,
        relax_rates,
        bin_element.reshape(1, bins),
        bin_fill.reshape(1, bins),
    )
    for turn in range(PASSES):
        last = turn == PASSES - 1
        halos = exchange(faces)
        q, *faces = pl.pallas_call(
            functools.partial(pass_kernel, last),
            out_shape=(field,) + (() if last else face_shapes),
            in_specs=[vmem] * 7,
            out_specs=(vmem,) * (1 if last else 5),
            compiler_params=params,
            name="advance",
        )(q, viscosity, axial_speed, *halos)
    return (q.reshape(3, NODES, sec_cells, air_cells), particles_out)


def solution(mesh):
    return jax.shard_map(
        local,
        mesh=mesh,
        in_specs=(
            P(None, None, "section", "airway"),
            P("section", "airway"),
            P("section", "airway"),
            P("section", "airway"),
            P(("airway", "section"), None, None),
            P(("airway", "section"), None, None),
            P(("airway", "section"), None),
            P(("airway", "section")),
            P(("airway", "section")),
        ),
        out_specs=(P(None, None, "section", "airway"), P(("airway", "section"), None, None)),
        check_vma=False,
    )
```

profile of v0, /device:TPU:1, one launch (start us, length us, event | category | flops | bytes accessed | tf_op | source)
XLA Modules:
  0.0 128.4 jit_solution(12312942499786115252)
XLA Ops:
  0.6 0.0 copy-start.2
  0.6 0.0 copy-start.1
  0.7 1.0 copy.11.positions
  1.7 1.0 copy.12.velocities
  2.7 0.0 copy-start
  2.7 1.4 %copy-done = f32[3,64,8,256]{3,2,1,0:T(8,128)S(1)} copy-done((f32[3,64,8,256]{3,2,1,0:T(8,128)S(1)}, f32[3,64,8,256]{3,2,1,0:T(8,128)}, u32[]{:S(2)}) %copy-start) | copy-done | bytes 1572888
  4.1 0.8 copy-done.3
  4.9 0.7 copy-done.4
  5.6 0.7 copy-done.5
  6.3 0.7 copy-done.6
  6.9 61.2 %particles.1 = (f32[3,4,4,4,8,256]{5,4,3,2,1,0:T(8,128)S(1)}, f32[96,6,128]{2,1,0:T(8,128)S(1)}, f32[8,128]{1,0:T(8,128)S(1)}, f32[8,128]{1,0:T(8,128)S(1)}, f32...) custom-call(f32[3,4,4,4,8,256]{5,4,3,2,1,0:T(8,128)S(1)} %bitcast.4, f32[8,256]{1,0:T(8,128)S(1)} %copy-done.4, ...), custom_call_target="tpu_custom_call" | custom-call | tf_op jit(solution)/shard_map/particles/pallas_call | solution.py:357
  68.1 1.3 %collective-permute-start.2 = (f32[3,16,256]{2,1,0:T(8,128)S(1)}, f32[3,16,256]{2,1,0:T(8,128)S(1)}, u32[]{:S(2)}, u32[]{:S(2)}) collective-permute-start(f32[3,16,256]{2,1,0:T(8,128)S(1)} %get-tuple-element.26), channel_id=1, source_target_pairs={{1,0},{2,1},{3,2},{4,3},{5,4},{6,5},{7,6},{9,8},{10,9},{11,10},{12... | collective-permute-start | bytes 147464 | tf_op jit(solution)/shard_map/ppermute | solution.py:320
  69.4 4.6 %collective-permute-start.3 = (f32[3,16,256]{2,1,0:T(8,128)S(1)}, f32[3,16,256]{2,1,0:T(8,128)S(1)}, u32[]{:S(2)}, u32[]{:S(2)}) collective-permute-start(f32[3,16,256]{2,1,0:T(8,128)S(1)} %get-tuple-element.27), channel_id=1, source_target_pairs={{0,1},{1,2},{2,3},{3,4},{4,5},{5,6},{6,7},{8,9},{9,10},{10,11},{11... | collective-permute-start | bytes 147464 | tf_op jit(solution)/shard_map/ppermute | solution.py:320
  74.0 2.9 %collective-permute-start = (f32[8,128]{1,0:T(8,128)S(1)}, f32[8,128]{1,0:T(8,128)S(1)}, u32[]{:S(2)}, u32[]{:S(2)}) collective-permute-start(f32[8,128]{1,0:T(8,128)S(1)} %get-tuple-element.24), channel_id=1, source_target_pairs={{8,0},{16,8},{24,16},{9,1},{17,9},{25,17},{10,2},{18,10},{26,18},{... | collective-permute-start | bytes 12296 | tf_op jit(solution)/shard_map/ppermute | solution.py:320
  76.9 3.6 %collective-permute-start.1 = (f32[8,128]{1,0:T(8,128)S(1)}, f32[8,128]{1,0:T(8,128)S(1)}, u32[]{:S(2)}, u32[]{:S(2)}) collective-permute-start(f32[8,128]{1,0:T(8,128)S(1)} %get-tuple-element.25), channel_id=1, source_target_pairs={{0,8},{8,16},{16,24},{1,9},{9,17},{17,25},{2,10},{10,18},{18,26},{... | collective-permute-start | bytes 12296 | tf_op jit(solution)/shard_map/ppermute | solution.py:320
  80.4 0.0 collective-permute-done.ha_after
  80.5 0.7 collective-permute-done.1.ha_before
  81.2 0.0 collective-permute-done.2.hs_after
  81.2 0.0 collective-permute-done.3.hs_before
  81.2 1.5 %advance.4 = (f32[3,4,4,4,8,256]{5,4,3,2,1,0:T(8,128)S(1)}, f32[8,128]{1,0:T(8,128)S(1)}, f32[8,128]{1,0:T(8,128)S(1)}, f32[3,16,256]{2,1,0:T(8,128)S(1)}, f32[3,16,256]{2,1,0:T(8,128)S(1)}) custom-call(f32[3,4,4,4,8,256]{5,4,3,2,1,0:T(8,128)S(1)} %get-tuple-element.23.q, f32[8,256]{1,0:T(8,128)S(1)} %copy-done.1, f32[8,256]{1,0:T(8,128)S(1)} %copy-done.2, ...), custom_call_target="tpu_custom_call" | custom-call | tf_op jit(solution)/shard_map/advance/pallas_call | solution.py:386
  82.7 1.3 %collective-permute-start.6 = (f32[3,16,256]{2,1,0:T(8,128)S(1)}, f32[3,16,256]{2,1,0:T(8,128)S(1)}, u32[]{:S(2)}, u32[]{:S(2)}) collective-permute-start(f32[3,16,256]{2,1,0:T(8,128)S(1)} %get-tuple-element.31), channel_id=1, source_target_pairs={{1,0},{2,1},{3,2},{4,3},{5,4},{6,5},{7,6},{9,8},{10,9},{11,10},{12... | collective-permute-start | bytes 147464 | tf_op jit(solution)/shard_map/ppermute | solution.py:320
  84.0 4.6 %collective-permute-start.7 = (f32[3,16,256]{2,1,0:T(8,128)S(1)}, f32[3,16,256]{2,1,0:T(8,128)S(1)}, u32[]{:S(2)}, u32[]{:S(2)}) collective-permute-start(f32[3,16,256]{2,1,0:T(8,128)S(1)} %get-tuple-element.32), channel_id=1, source_target_pairs={{0,1},{1,2},{2,3},{3,4},{4,5},{5,6},{6,7},{8,9},{9,10},{10,11},{11... | collective-permute-start | bytes 147464 | tf_op jit(solution)/shard_map/ppermute | solution.py:320
  88.6 1.9 %collective-permute-start.4 = (f32[8,128]{1,0:T(8,128)S(1)}, f32[8,128]{1,0:T(8,128)S(1)}, u32[]{:S(2)}, u32[]{:S(2)}) collective-permute-start(f32[8,128]{1,0:T(8,128)S(1)} %get-tuple-element.29), channel_id=1, source_target_pairs={{8,0},{16,8},{24,16},{9,1},{17,9},{25,17},{10,2},{18,10},{26,18},{... | collective-permute-start | bytes 12296 | tf_op jit(solution)/shard_map/ppermute | solution.py:320
  90.6 4.5 %collective-permute-start.5 = (f32[8,128]{1,0:T(8,128)S(1)}, f32[8,128]{1,0:T(8,128)S(1)}, u32[]{:S(2)}, u32[]{:S(2)}) collective-permute-start(f32[8,128]{1,0:T(8,128)S(1)} %get-tuple-element.30), channel_id=1, source_target_pairs={{0,8},{8,16},{16,24},{1,9},{9,17},{17,25},{2,10},{10,18},{18,26},{... | collective-permute-start | bytes 12296 | tf_op jit(solution)/shard_map/ppermute | solution.py:320
  95.0 0.0 collective-permute-done.4.ha_after
  95.0 0.7 collective-permute-done.5.ha_before
  95.8 0.0 collective-permute-done.6.hs_after
  95.8 0.0 collective-permute-done.7.hs_before
  95.8 1.5 %advance.5 = (f32[3,4,4,4,8,256]{5,4,3,2,1,0:T(8,128)S(1)}, f32[8,128]{1,0:T(8,128)S(1)}, f32[8,128]{1,0:T(8,128)S(1)}, f32[3,16,256]{2,1,0:T(8,128)S(1)}, f32[3,16,256]{2,1,0:T(8,128)S(1)}) custom-call(f32[3,4,4,4,8,256]{5,4,3,2,1,0:T(8,128)S(1)} %get-tuple-element.28.q, f32[8,256]{1,0:T(8,128)S(1)} %copy-done.1, f32[8,256]{1,0:T(8,128)S(1)} %copy-done.2, ...), custom_call_target="tpu_custom_call" | custom-call | tf_op jit(solution)/shard_map/advance/pallas_call | solution.py:386
  97.2 1.3 %collective-permute-start.10 = (f32[3,16,256]{2,1,0:T(8,128)S(1)}, f32[3,16,256]{2,1,0:T(8,128)S(1)}, u32[]{:S(2)}, u32[]{:S(2)}) collective-permute-start(f32[3,16,256]{2,1,0:T(8,128)S(1)} %get-tuple-element.36), channel_id=1, source_target_pairs={{1,0},{2,1},{3,2},{4,3},{5,4},{6,5},{7,6},{9,8},{10,9},{11,10},{12... | collective-permute-start | bytes 147464 | tf_op jit(solution)/shard_map/ppermute | solution.py:320
  98.5 5.2 %collective-permute-start.11 = (f32[3,16,256]{2,1,0:T(8,128)S(1)}, f32[3,16,256]{2,1,0:T(8,128)S(1)}, u32[]{:S(2)}, u32[]{:S(2)}) collective-permute-start(f32[3,16,256]{2,1,0:T(8,128)S(1)} %get-tuple-element.37), channel_id=1, source_target_pairs={{0,1},{1,2},{2,3},{3,4},{4,5},{5,6},{6,7},{8,9},{9,10},{10,11},{11... | collective-permute-start | bytes 147464 | tf_op jit(solution)/shard_map/ppermute | solution.py:320
  103.7 1.9 %collective-permute-start.8 = (f32[8,128]{1,0:T(8,128)S(1)}, f32[8,128]{1,0:T(8,128)S(1)}, u32[]{:S(2)}, u32[]{:S(2)}) collective-permute-start(f32[8,128]{1,0:T(8,128)S(1)} %get-tuple-element.34), channel_id=1, source_target_pairs={{8,0},{16,8},{24,16},{9,1},{17,9},{25,17},{10,2},{18,10},{26,18},{... | collective-permute-start | bytes 12296 | tf_op jit(solution)/shard_map/ppermute | solution.py:320
  105.6 4.5 %collective-permute-start.9 = (f32[8,128]{1,0:T(8,128)S(1)}, f32[8,128]{1,0:T(8,128)S(1)}, u32[]{:S(2)}, u32[]{:S(2)}) collective-permute-start(f32[8,128]{1,0:T(8,128)S(1)} %get-tuple-element.35), channel_id=1, source_target_pairs={{0,8},{8,16},{16,24},{1,9},{9,17},{17,25},{2,10},{10,18},{18,26},{... | collective-permute-start | bytes 12296 | tf_op jit(solution)/shard_map/ppermute | solution.py:320
  110.1 0.0 collective-permute-done.8.ha_after
  110.1 0.7 collective-permute-done.9.ha_before
  110.9 0.0 collective-permute-done.10.hs_after
  110.9 0.0 collective-permute-done.11.hs_before
  110.9 1.5 %advance.6 = (f32[3,4,4,4,8,256]{5,4,3,2,1,0:T(8,128)S(1)}, f32[8,128]{1,0:T(8,128)S(1)}, f32[8,128]{1,0:T(8,128)S(1)}, f32[3,16,256]{2,1,0:T(8,128)S(1)}, f32[3,16,256]{2,1,0:T(8,128)S(1)}) custom-call(f32[3,4,4,4,8,256]{5,4,3,2,1,0:T(8,128)S(1)} %get-tuple-element.33.q, f32[8,256]{1,0:T(8,128)S(1)} %copy-done.1, f32[8,256]{1,0:T(8,128)S(1)} %copy-done.2, ...), custom_call_target="tpu_custom_call" | custom-call | tf_op jit(solution)/shard_map/advance/pallas_call | solution.py:386
  112.3 1.3 %collective-permute-start.14 = (f32[3,16,256]{2,1,0:T(8,128)S(1)}, f32[3,16,256]{2,1,0:T(8,128)S(1)}, u32[]{:S(2)}, u32[]{:S(2)}) collective-permute-start(f32[3,16,256]{2,1,0:T(8,128)S(1)} %get-tuple-element.41), channel_id=1, source_target_pairs={{1,0},{2,1},{3,2},{4,3},{5,4},{6,5},{7,6},{9,8},{10,9},{11,10},{12... | collective-permute-start | bytes 147464 | tf_op jit(solution)/shard_map/ppermute | solution.py:320
  113.6 5.2 %collective-permute-start.15 = (f32[3,16,256]{2,1,0:T(8,128)S(1)}, f32[3,16,256]{2,1,0:T(8,128)S(1)}, u32[]{:S(2)}, u32[]{:S(2)}) collective-permute-start(f32[3,16,256]{2,1,0:T(8,128)S(1)} %get-tuple-element.42), channel_id=1, source_target_pairs={{0,1},{1,2},{2,3},{3,4},{4,5},{5,6},{6,7},{8,9},{9,10},{10,11},{11... | collective-permute-start | bytes 147464 | tf_op jit(solution)/shard_map/ppermute | solution.py:320
  118.8 1.9 %collective-permute-start.12 = (f32[8,128]{1,0:T(8,128)S(1)}, f32[8,128]{1,0:T(8,128)S(1)}, u32[]{:S(2)}, u32[]{:S(2)}) collective-permute-start(f32[8,128]{1,0:T(8,128)S(1)} %get-tuple-element.39), channel_id=1, source_target_pairs={{8,0},{16,8},{24,16},{9,1},{17,9},{25,17},{10,2},{18,10},{26,18},{... | collective-permute-start | bytes 12296 | tf_op jit(solution)/shard_map/ppermute | solution.py:320
  120.7 4.5 %collective-permute-start.13 = (f32[8,128]{1,0:T(8,128)S(1)}, f32[8,128]{1,0:T(8,128)S(1)}, u32[]{:S(2)}, u32[]{:S(2)}) collective-permute-start(f32[8,128]{1,0:T(8,128)S(1)} %get-tuple-element.40), channel_id=1, source_target_pairs={{0,8},{8,16},{16,24},{1,9},{9,17},{17,25},{2,10},{10,18},{18,26},{... | collective-permute-start | bytes 12296 | tf_op jit(solution)/shard_map/ppermute | solution.py:320
  125.2 0.8 copy.13
  126.0 0.0 collective-permute-done.12.ha_after
  126.0 0.0 collective-permute-done.13.ha_before
  126.0 0.0 collective-permute-done.14.hs_after
  126.0 0.0 collective-permute-done.15.hs_before
  126.0 2.5 %advance.7 = f32[3,4,4,4,8,256]{5,4,3,2,1,0:T(8,128)} custom-call(f32[3,4,4,4,8,256]{5,4,3,2,1,0:T(8,128)S(1)} %get-tuple-element.38.q, f32[8,256]{1,0:T(8,128)S(1)} %copy-done.1, f32[8,256]{1,0:T(8,128)S(1)} %copy-done.2, f32[8,128]{1,0:T(8,128)S(1)} %collective-permute-done.12.ha_after, f32[8,128]{1,0:T(8,128)S(1)} %collective-permute-done.13.ha_before, ...), custom_call_target="tpu_custom_call" | custom-call | tf_op jit(solution)/shard_map/advance/pallas_call | solution.py:386
  (6 shorter events, 0.0 us)
Async XLA Ops:
  0.6 80.6 %copy-start.2 = (f32[8,256]{1,0:T(8,128)S(1)}, f32[8,256]{1,0:T(8,128)}, u32[]{:S(2)}) copy-start(f32[8,256]{1,0:T(8,128)} %speed.7) | copy-start | bytes 24580
  0.6 80.6 %copy-start.1 = (f32[8,256]{1,0:T(8,128)S(1)}, f32[8,256]{1,0:T(8,128)}, u32[]{:S(2)}) copy-start(f32[8,256]{1,0:T(8,128)} %visc.7) | copy-start | bytes 24580
  2.7 1.4 %copy-start = (f32[3,64,8,256]{3,2,1,0:T(8,128)S(1)}, f32[3,64,8,256]{3,2,1,0:T(8,128)}, u32[]{:S(2)}) copy-start(f32[3,64,8,256]{3,2,1,0:T(8,128)} %param.9) | copy-start | bytes 4718596
  4.1 0.8 copy-start.3
  4.9 0.7 copy-start.4
  5.6 0.7 copy-start.5
  6.3 0.7 copy-start.6
  68.1 13.0 %collective-permute-start.2 = (f32[3,16,256]{2,1,0:T(8,128)S(1)}, f32[3,16,256]{2,1,0:T(8,128)S(1)}, u32[]{:S(2)}, u32[]{:S(2)}) collective-permute-start(f32[3,16,256]{2,1,0:T(8,128)S(1)} %get-tuple-element.26), channel_id=1, source_target_pairs={{1,0},{2,1},{3,2},{4,3},{5,4},{6,5},{7,6},{9,8},{10,9},{11,10},{12... | collective-permute-start | bytes 147464 | tf_op jit(solution)/shard_map/ppermute | solution.py:320
  69.4 11.8 %collective-permute-start.3 = (f32[3,16,256]{2,1,0:T(8,128)S(1)}, f32[3,16,256]{2,1,0:T(8,128)S(1)}, u32[]{:S(2)}, u32[]{:S(2)}) collective-permute-start(f32[3,16,256]{2,1,0:T(8,128)S(1)} %get-tuple-element.27), channel_id=1, source_target_pairs={{0,1},{1,2},{2,3},{3,4},{4,5},{5,6},{6,7},{8,9},{9,10},{10,11},{11... | collective-permute-start | bytes 147464 | tf_op jit(solution)/shard_map/ppermute | solution.py:320
  74.0 6.4 %collective-permute-start = (f32[8,128]{1,0:T(8,128)S(1)}, f32[8,128]{1,0:T(8,128)S(1)}, u32[]{:S(2)}, u32[]{:S(2)}) collective-permute-start(f32[8,128]{1,0:T(8,128)S(1)} %get-tuple-element.24), channel_id=1, source_target_pairs={{8,0},{16,8},{24,16},{9,1},{17,9},{25,17},{10,2},{18,10},{26,18},{... | collective-permute-start | bytes 12296 | tf_op jit(solution)/shard_map/ppermute | solution.py:320
  76.9 4.3 %collective-permute-start.1 = (f32[8,128]{1,0:T(8,128)S(1)}, f32[8,128]{1,0:T(8,128)S(1)}, u32[]{:S(2)}, u32[]{:S(2)}) collective-permute-start(f32[8,128]{1,0:T(8,128)S(1)} %get-tuple-element.25), channel_id=1, source_target_pairs={{0,8},{8,16},{16,24},{1,9},{9,17},{17,25},{2,10},{10,18},{18,26},{... | collective-permute-start | bytes 12296 | tf_op jit(solution)/shard_map/ppermute | solution.py:320
  82.7 13.1 %collective-permute-start.6 = (f32[3,16,256]{2,1,0:T(8,128)S(1)}, f32[3,16,256]{2,1,0:T(8,128)S(1)}, u32[]{:S(2)}, u32[]{:S(2)}) collective-permute-start(f32[3,16,256]{2,1,0:T(8,128)S(1)} %get-tuple-element.31), channel_id=1, source_target_pairs={{1,0},{2,1},{3,2},{4,3},{5,4},{6,5},{7,6},{9,8},{10,9},{11,10},{12... | collective-permute-start | bytes 147464 | tf_op jit(solution)/shard_map/ppermute | solution.py:320
  84.0 11.8 %collective-permute-start.7 = (f32[3,16,256]{2,1,0:T(8,128)S(1)}, f32[3,16,256]{2,1,0:T(8,128)S(1)}, u32[]{:S(2)}, u32[]{:S(2)}) collective-permute-start(f32[3,16,256]{2,1,0:T(8,128)S(1)} %get-tuple-element.32), channel_id=1, source_target_pairs={{0,1},{1,2},{2,3},{3,4},{4,5},{5,6},{6,7},{8,9},{9,10},{10,11},{11... | collective-permute-start | bytes 147464 | tf_op jit(solution)/shard_map/ppermute | solution.py:320
  88.6 6.4 %collective-permute-start.4 = (f32[8,128]{1,0:T(8,128)S(1)}, f32[8,128]{1,0:T(8,128)S(1)}, u32[]{:S(2)}, u32[]{:S(2)}) collective-permute-start(f32[8,128]{1,0:T(8,128)S(1)} %get-tuple-element.29), channel_id=1, source_target_pairs={{8,0},{16,8},{24,16},{9,1},{17,9},{25,17},{10,2},{18,10},{26,18},{... | collective-permute-start | bytes 12296 | tf_op jit(solution)/shard_map/ppermute | solution.py:320
  90.6 5.2 %collective-permute-start.5 = (f32[8,128]{1,0:T(8,128)S(1)}, f32[8,128]{1,0:T(8,128)S(1)}, u32[]{:S(2)}, u32[]{:S(2)}) collective-permute-start(f32[8,128]{1,0:T(8,128)S(1)} %get-tuple-element.30), channel_id=1, source_target_pairs={{0,8},{8,16},{16,24},{1,9},{9,17},{17,25},{2,10},{10,18},{18,26},{... | collective-permute-start | bytes 12296 | tf_op jit(solution)/shard_map/ppermute | solution.py:320
  97.2 13.6 %collective-permute-start.10 = (f32[3,16,256]{2,1,0:T(8,128)S(1)}, f32[3,16,256]{2,1,0:T(8,128)S(1)}, u32[]{:S(2)}, u32[]{:S(2)}) collective-permute-start(f32[3,16,256]{2,1,0:T(8,128)S(1)} %get-tuple-element.36), channel_id=1, source_target_pairs={{1,0},{2,1},{3,2},{4,3},{5,4},{6,5},{7,6},{9,8},{10,9},{11,10},{12... | collective-permute-start | bytes 147464 | tf_op jit(solution)/shard_map/ppermute | solution.py:320
  98.5 12.3 %collective-permute-start.11 = (f32[3,16,256]{2,1,0:T(8,128)S(1)}, f32[3,16,256]{2,1,0:T(8,128)S(1)}, u32[]{:S(2)}, u32[]{:S(2)}) collective-permute-start(f32[3,16,256]{2,1,0:T(8,128)S(1)} %get-tuple-element.37), channel_id=1, source_target_pairs={{0,1},{1,2},{2,3},{3,4},{4,5},{5,6},{6,7},{8,9},{9,10},{10,11},{11... | collective-permute-start | bytes 147464 | tf_op jit(solution)/shard_map/ppermute | solution.py:320
  103.7 6.4 %collective-permute-start.8 = (f32[8,128]{1,0:T(8,128)S(1)}, f32[8,128]{1,0:T(8,128)S(1)}, u32[]{:S(2)}, u32[]{:S(2)}) collective-permute-start(f32[8,128]{1,0:T(8,128)S(1)} %get-tuple-element.34), channel_id=1, source_target_pairs={{8,0},{16,8},{24,16},{9,1},{17,9},{25,17},{10,2},{18,10},{26,18},{... | collective-permute-start | bytes 12296 | tf_op jit(solution)/shard_map/ppermute | solution.py:320
  105.6 5.2 %collective-permute-start.9 = (f32[8,128]{1,0:T(8,128)S(1)}, f32[8,128]{1,0:T(8,128)S(1)}, u32[]{:S(2)}, u32[]{:S(2)}) collective-permute-start(f32[8,128]{1,0:T(8,128)S(1)} %get-tuple-element.35), channel_id=1, source_target_pairs={{0,8},{8,16},{16,24},{1,9},{9,17},{17,25},{2,10},{10,18},{18,26},{... | collective-permute-start | bytes 12296 | tf_op jit(solution)/shard_map/ppermute | solution.py:320
  112.3 13.7 %collective-permute-start.14 = (f32[3,16,256]{2,1,0:T(8,128)S(1)}, f32[3,16,256]{2,1,0:T(8,128)S(1)}, u32[]{:S(2)}, u32[]{:S(2)}) collective-permute-start(f32[3,16,256]{2,1,0:T(8,128)S(1)} %get-tuple-element.41), channel_id=1, source_target_pairs={{1,0},{2,1},{3,2},{4,3},{5,4},{6,5},{7,6},{9,8},{10,9},{11,10},{12... | collective-permute-start | bytes 147464 | tf_op jit(solution)/shard_map/ppermute | solution.py:320
  113.6 12.4 %collective-permute-start.15 = (f32[3,16,256]{2,1,0:T(8,128)S(1)}, f32[3,16,256]{2,1,0:T(8,128)S(1)}, u32[]{:S(2)}, u32[]{:S(2)}) collective-permute-start(f32[3,16,256]{2,1,0:T(8,128)S(1)} %get-tuple-element.42), channel_id=1, source_target_pairs={{0,1},{1,2},{2,3},{3,4},{4,5},{5,6},{6,7},{8,9},{9,10},{10,11},{11... | collective-permute-start | bytes 147464 | tf_op jit(solution)/shard_map/ppermute | solution.py:320
  118.8 7.2 %collective-permute-start.12 = (f32[8,128]{1,0:T(8,128)S(1)}, f32[8,128]{1,0:T(8,128)S(1)}, u32[]{:S(2)}, u32[]{:S(2)}) collective-permute-start(f32[8,128]{1,0:T(8,128)S(1)} %get-tuple-element.39), channel_id=1, source_target_pairs={{8,0},{16,8},{24,16},{9,1},{17,9},{25,17},{10,2},{18,10},{26,18},{... | collective-permute-start | bytes 12296 | tf_op jit(solution)/shard_map/ppermute | solution.py:320
  120.7 5.2 %collective-permute-start.13 = (f32[8,128]{1,0:T(8,128)S(1)}, f32[8,128]{1,0:T(8,128)S(1)}, u32[]{:S(2)}, u32[]{:S(2)}) collective-permute-start(f32[8,128]{1,0:T(8,128)S(1)} %get-tuple-element.40), channel_id=1, source_target_pairs={{0,8},{8,16},{16,24},{1,9},{9,17},{17,25},{2,10},{10,18},{18,26},{... | collective-permute-start | bytes 12296 | tf_op jit(solution)/shard_map/ppermute | solution.py:320
where the time goes:
time: 130 us; the launch traced here: 128 us
  Pallas kernels  68.1 us (52%)
  starting transfers between devices  50.3 us (39%)
  local copies, waits for them, and re-layouts  7.02 us (5%)
  waiting for transfers between devices  2.2 us (2%)
    pallas_call x1, Pallas kernels, local(): pl.pallas_call(particle_kernel, out_shape=(field, jax.ShapeDtypeStruct((b...  61.2 us
    ppermute x16, starting transfers between devices, shift(): return lax.ppermute(values, axis, pairs)  50.3 us
    unnamed x17, local copies, waits for them, and re-layouts  7.02 us
    pallas_call x4, Pallas kernels, local(): pl.pallas_call(functools.partial(pass_kernel, last), out_shape=(field,) +...  6.85 us
  transfers between devices with their start and end apart: 16, of which 3 were waited for; matrix products, arithmetic and copies ran while one was open for 1% of the time, Pallas kernels for 0%

commit v1 on v0

--- a/solution.py
+++ b/solution.py
@@ -49,7 +49,11 @@
     return [outer - outer_x, third - inner_x, third + inner_x, outer + outer_x]
 
 
-def send_faces(q, sa_next, sa_prev, ss_next, ss_prev):
+def is_even(axis):
+    return lax.axis_index(axis) % 2 == 0
+
+
+def send_faces(q, sa_first, sa_second, ss_first, ss_second):
     cells = q.shape[-1]
     lane = iota((SUB, LANE), 1)
     nxt = jnp.zeros((SUB, LANE), f32)
@@ -62,14 +66,18 @@
                 head = q[comp, 0, b, c, :, :LANE]
                 nxt = jnp.where(lane == i, pltpu.roll(tail, (i + 1) % LANE, 1), nxt)
                 prv = jnp.where(lane == i, pltpu.roll(head, i, 1), prv)
-    sa_next[...] = nxt
-    sa_prev[...] = prv
+    even = is_even("airway")
+    sa_first[...] = jnp.where(even, nxt, prv)
+    sa_second[...] = jnp.where(even, prv, nxt)
+    even = is_even("section")
     for comp in range(3):
         for a in range(4):
             for c in range(4):
                 i = a * 4 + c
-                ss_next[comp, i : i + 1, :] = q[comp, a, 3, c, SUB - 1 : SUB, :]
-                ss_prev[comp, i : i + 1, :] = q[comp, a, 0, c, 0:1, :]
+                tail = q[comp, a, 3, c, SUB - 1 : SUB, :]
+                head = q[comp, a, 0, c, 0:1, :]
+                ss_first[comp, i : i + 1, :] = jnp.where(even, tail, head)
+                ss_second[comp, i : i + 1, :] = jnp.where(even, head, tail)
 
 
 def second_line(q, v_even, v_odd):
@@ -79,7 +87,7 @@
     return [even - odd, even - third, even + third, even + odd]
 
 
-def pass_kernel(last, q, visc, speed, ha_after, ha_before, hs_after, hs_before, out, *sends):
+def pass_kernel(last, q, visc, speed, ha_first, ha_second, hs_first, hs_second, out, *sends):
     cells = q.shape[-1]
     tiles = cells // LANE
     lane = iota((SUB, LANE), 1)
@@ -90,8 +98,10 @@
     is_first_row = row == 0
 
     def component(comp, carry):
-        halo_after = ha_after[...]
-        halo_before = ha_before[...]
+        forward = is_even("airway")
+        halo_after = jnp.where(forward, ha_first[...], ha_second[...])
+        halo_before = jnp.where(forward, ha_second[...], ha_first[...])
+        forward = is_even("section")
         for j in range(tiles):
             at = pl.ds(j * LANE, LANE)
             v_even = visc[:, at] * 1.125
@@ -143,14 +153,17 @@
                 for c in range(4):
                     line = [q[comp, a, b, c, :, at] for b in range(4)]
                     new = second_line(line, v_even, v_odd)
+                    i = a * 4 + c
+                    first = jnp.broadcast_to(hs_first[comp, i : i + 1, at], (SUB, LANE))
+                    second = jnp.broadcast_to(hs_second[comp, i : i + 1, at], (SUB, LANE))
                     after = jnp.where(
                         is_last_row,
-                        jnp.broadcast_to(hs_after[comp, a * 4 + c : a * 4 + c + 1, at], (SUB, LANE)),
+                        jnp.where(forward, first, second),
                         pltpu.roll(line[0], SUB - 1, 0),
                     )
                     before = jnp.where(
                         is_first_row,
-                        jnp.broadcast_to(hs_before[comp, a * 4 + c : a * 4 + c + 1, at], (SUB, LANE)),
+                        jnp.where(forward, second, first),
                         pltpu.roll(line[3], 1, 0),
                     )
                     new[3] = new[3] + penalty_weight * (after - line[3])
@@ -165,35 +178,60 @@
 
 
 def particle_kernel(
-    fluid,
-    mass,
+    fluid_hbm,
+    mass_hbm,
     positions,
     velocities,
-    relax,
-    element_row,
-    fill_row,
+    relax_hbm,
+    element_hbm,
+    fill_hbm,
     q_out,
     parts_out,
-    sa_next,
-    sa_prev,
-    ss_next,
-    ss_prev,
-    state,
+    sa_first,
+    sa_second,
+    ss_first,
+    ss_second,
     rates,
     strides,
     occupied,
     nodal,
     sums,
+    totals,
     one_hot,
     rows_ref,
+    fluid,
+    mass,
+    relax,
+    element_row,
+    fill_row,
+    arrived,
 ):
-    bins = positions.shape[0]
+    copies = [
+        pltpu.make_async_copy(source, target, arrived.at[i])
+        for i, (source, target) in enumerate(
+            (
+                (element_hbm, element_row),
+                (fill_hbm, fill_row),
+                (fluid_hbm, fluid),
+                (relax_hbm, relax),
+                (positions, parts_out.at[0:3]),
+                (velocities, parts_out.at[3:6]),
+                (mass_hbm, mass),
+            )
+        )
+    ]
+    for copy in copies:
+        copy.start()
+    bins = positions.shape[1]
     groups = bins // SUB
     lanes_bins = one_hot.shape[0]
     cells = fluid.shape[-1]
     row8 = iota((SUB, LANE), 0)
     lane8 = iota((SUB, LANE), 1)
     same = (lane8 % SUB == row8).astype(f32)
+
+    copies[0].wait()
+    copies[1].wait()
 
     rows_ref[...] = jnp.full(rows_ref.shape, -1.0, f32)
     rows_ref[0:1, :bins] = element_row[...].astype(f32)
@@ -219,13 +257,11 @@
         at = pl.ds(g * SUB, SUB)
         occ = (lane8.astype(f32) < fill).astype(f32)
         occupied[at, :] = occ
-        rates[at, :] = relax[at, :] * occ
         strides[at, :] = occ * stride_step
-        for k in range(3):
-            state[k, at, :] = positions[at, k, :]
-            state[3 + k, at, :] = velocities[at, k, :]
         hot = (iota((SUB, cells), 1).astype(f32) == column).astype(f32)
         one_hot[at, :] = hot.astype(bf16)
+
+    copies[2].wait()
 
     spread = (iota((LANE, LANE), 0) // SUB == iota((LANE, LANE), 1) // SUB).astype(bf16)
     section_col = jnp.concatenate(section_cols, axis=0)
@@ -239,94 +275,108 @@
                 picked = jnp.where(in_section, dot_t(hot_bins, source), 0.0).astype(bf16)
                 wide = dot(picked, spread)
                 for g in range(groups):
-                    block = (wide[g * SUB : (g + 1) * SUB, :] * same).astype(f32)
-                    nodal[g, part, i * SUB : (i + 1) * SUB, :] = block.astype(bf16)
-
-    sums[...] = jnp.zeros(sums.shape, f32)
+                    block = wide[g * SUB : (g + 1) * SUB, :] * same
+                    nodal[g, part * 96 + i * SUB : part * 96 + (i + 1) * SUB, :] = block.astype(bf16)
+
+    for copy in copies[3:]:
+        copy.wait()
+    rates[...] = relax[...] * occupied[...]
+    totals[...] = jnp.zeros(totals.shape, f32)
 
     def substep(first, turn, carry):
-        for g in range(first, first + GROUPS_TOGETHER):
+        for slot in range(GROUPS_TOGETHER):
+            g = first + slot
             at = pl.ds(g * SUB, SUB)
-            x = [state[k, at, :] for k in range(3)]
-            v = [state[3 + k, at, :] for k in range(3)]
+            x = [parts_out[k, at, :] for k in range(3)]
+            v = [parts_out[3 + k, at, :] for k in range(3)]
             rate = rates[at, :]
             step = strides[at, :]
             occ = occupied[at, :]
             la, lb, lc = [basis_values(x[k]) for k in range(3)]
-            across = jnp.concatenate([lb[b] * lc[c] for b in range(4) for c in range(4)], axis=0)
-            high, low = split(across)
-            n_high = nodal[g, 0]
-            n_low = nodal[g, 1]
-            at_a = dot(n_high, high) + (dot(n_high, low) + dot(n_low, high))
+            across = [lb[b] * lc[c] for b in range(4) for c in range(4)]
+            high, low = split(jnp.concatenate(across, axis=0))
+            by_high = dot(nodal[g], high)
+            at_a = by_high[:96] + (by_high[96:] + dot(nodal[g, :96], low))
             pushes = []
             for k in range(3):
                 rows = [at_a[(k * 4 + a) * SUB : (k * 4 + a + 1) * SUB, :] for a in range(4)]
                 u = (la[0] * rows[0] + la[1] * rows[1]) + (la[2] * rows[2] + la[3] * rows[3])
                 dv = rate * (u - v[k])
                 moved = v[k] + dv
-                state[3 + k, at, :] = moved
-                state[k, at, :] = jnp.clip(x[k] + step * moved, -1.0, 1.0)
+                parts_out[3 + k, at, :] = moved
+                parts_out[k, at, :] = jnp.clip(x[k] + step * moved, -1.0, 1.0)
                 pushes += [la[a] * dv for a in range(4)]
-            push_high, push_low = split(jnp.concatenate(pushes, axis=0))
-            drag = dot_t(push_high, high) + (dot_t(push_high, low) + dot_t(push_low, high))
-            square_high, square_low = split(across * across)
-            weigh_high, weigh_low = split(
-                jnp.concatenate([la[a] * la[a] * occ for a in range(4)], axis=0)
-            )
-            weight = dot_t(weigh_high, square_high) + (
-                dot_t(weigh_high, square_low) + dot_t(weigh_low, square_high)
-            )
-            sums[g] = sums[g] + jnp.concatenate([drag, weight], axis=0)
+            weighs = [la[a] * la[a] * occ for a in range(4)]
+            for n in range(16):
+                for i in range(12):
+                    j = i * 16 + n
+                    sums[slot, j] = sums[slot, j] + across[n] * pushes[i]
+            for n in range(16):
+                square = across[n] * across[n]
+                for a in range(4):
+                    j = (12 + a) * 16 + n
+                    sums[slot, j] = sums[slot, j] + square * weighs[a]
         return carry
 
+    def over_lanes(slot, start):
+        terms = [sums[slot, start + n] for n in range(LANE)]
+        width = 1
+        while width < LANE:
+            upper = (lane8 // width) % 2 == 1
+            terms = [
+                jnp.where(upper, odd, even) + pltpu.roll(jnp.where(upper, even, odd), width, 1)
+                for even, odd in zip(terms[0::2], terms[1::2])
+            ]
+            width *= 2
+        return terms[0]
+
     for first in range(0, groups, GROUPS_TOGETHER):
+        sums[...] = jnp.zeros(sums.shape, f32)
         lax.fori_loop(0, SUBSTEPS, functools.partial(substep, first), 0)
-
-    for g in range(groups):
-        at = pl.ds(g * SUB, SUB)
-        for k in range(6):
-            parts_out[at, k, :] = state[k, at, :]
+        for slot in range(GROUPS_TOGETHER):
+            at = pl.ds((first + slot) * SUB, SUB)
+            totals[at, :LANE] = over_lanes(slot, 0)
+            totals[at, LANE:] = over_lanes(slot, LANE)
 
     in_section_rows = (iota((LANE, lanes_bins), 0) % SUB).astype(f32) == section_lanes
     hot_all = one_hot[...]
-    spread2 = spread
-
-    def deposit(i):
-        blocks = [sums[g, i * SUB : (i + 1) * SUB, :] * same for g in range(groups)]
-        blocks += [jnp.zeros((SUB, LANE), f32)] * (lanes_bins // SUB - groups)
-        high, low = split(jnp.concatenate(blocks, axis=0))
-        wide = dot_t(spread2, high) + dot_t(spread2, low)
-        wide = jnp.where(in_section_rows, wide, 0.0)
-        high, low = split(wide)
-        return dot(high, hot_all) + dot(low, hot_all)
+    spread_rows = (iota((LANE, 16), 0) // SUB == iota((LANE, 16), 1)).astype(bf16)
+    by_node = jnp.concatenate([totals[:, :LANE].T, totals[:, LANE:].T], axis=0)
 
     for a in range(4):
-        weight = deposit(12 + a).reshape(4, 4, SUB, cells)
-        scale = 1.0 / (mass[...][None, None] + weight)
+        highs = []
+        lows = []
+        for i in (12 + a, a, 4 + a, 8 + a):
+            high, low = split(by_node[i * 16 : (i + 1) * 16, :])
+            wide = dot(spread_rows, high) + dot(spread_rows, low)
+            high, low = split(jnp.where(in_section_rows, wide, 0.0))
+            highs.append(high)
+            lows.append(low)
+        placed = dot(jnp.concatenate(highs + lows, axis=0), hot_all)
+        placed = (placed[: 4 * LANE] + placed[4 * LANE :]).reshape(4, 4, 4, SUB, cells)
+        scale = 1.0 / (mass[...][None, None] + placed[0])
         for comp in range(3):
-            drag = deposit(comp * 4 + a).reshape(4, 4, SUB, cells)
-            q_out[comp, a] = fluid[comp, a] - drag * scale
-
-    send_faces(q_out, sa_next, sa_prev, ss_next, ss_prev)
-
-
-def shift(values, axis, up):
+            q_out[comp, a] = fluid[comp, a] - placed[1 + comp] * scale
+
+    send_faces(q_out, sa_first, sa_second, ss_first, ss_second)
+
+
+def swap(values, axis, offset):
     count = lax.axis_size(axis)
-    ends = count - 1
-    if up:
-        pairs = [(i, i + 1) for i in range(ends)]
-    else:
-        pairs = [(i + 1, i) for i in range(ends)]
+    pairs = []
+    for i in range(offset, count - 1, 2):
+        pairs += [(i, i + 1), (i + 1, i)]
     return lax.ppermute(values, axis, pairs)
 
 
 def exchange(faces):
-    sa_next, sa_prev, ss_next, ss_prev = faces
-    ha_before = shift(sa_next, "airway", True)
-    ha_after = shift(sa_prev, "airway", False)
-    hs_before = shift(ss_next, "section", True)
-    hs_after = shift(ss_prev, "section", False)
-    return ha_after, ha_before, hs_after, hs_before
+    sa_first, sa_second, ss_first, ss_second = faces
+    return (
+        swap(sa_first, "airway", 0),
+        swap(sa_second, "airway", 1),
+        swap(ss_first, "section", 0),
+        swap(ss_second, "section", 1),
+    )
 
 
 def local(
@@ -353,32 +403,44 @@
         jax.ShapeDtypeStruct((3, 16, air_cells), f32),
     )
     vmem = pl.BlockSpec(memory_space=pltpu.VMEM)
+    hbm = pl.BlockSpec(memory_space=pltpu.HBM)
     params = pltpu.CompilerParams(vmem_limit_bytes=48 * 1024 * 1024)
     q, particles_out, *faces = pl.pallas_call(
         particle_kernel,
-        out_shape=(field, jax.ShapeDtypeStruct((bins, 6, LANE), f32)) + face_shapes,
-        in_specs=[vmem] * 7,
+        out_shape=(field, jax.ShapeDtypeStruct((6, bins, LANE), f32)) + face_shapes,
+        in_specs=[hbm] * 7,
         out_specs=(vmem,) * 6,
         scratch_shapes=[
-            pltpu.VMEM((6, bins, LANE), f32),
             pltpu.VMEM((bins, LANE), f32),
             pltpu.VMEM((bins, LANE), f32),
             pltpu.VMEM((bins, LANE), f32),
-            pltpu.VMEM((groups, 2, 96, LANE), bf16),
-            pltpu.VMEM((groups, LANE, LANE), f32),
+            pltpu.VMEM((groups, 192, LANE), bf16),
+            pltpu.VMEM((GROUPS_TOGETHER, 256, SUB, LANE), f32),
+            pltpu.VMEM((lanes_bins, 256), f32),
             pltpu.VMEM((lanes_bins, air_cells), bf16),
             pltpu.VMEM((SUB, lanes_bins), f32),
+            pltpu.VMEM(field_shape, f32),
+            pltpu.VMEM(fluid_mass.shape, f32),
+            pltpu.VMEM(relax_rates.shape, f32),
+            pltpu.VMEM((1, bins), jnp.int32),
+            pltpu.VMEM((1, bins), jnp.int32),
+            pltpu.SemaphoreType.DMA((7,)),
         ],
         compiler_params=params,
         name="particles",
     )(
-        fluid_velocity.reshape(field_shape),
-        fluid_mass,
-        positions,
-        velocities,
-        relax_rates,
-        bin_element.reshape(1, bins),
-        bin_fill.reshape(1, bins),
+        *(
+            pltpu.with_memory_space_constraint(array, pltpu.HBM)
+            for array in (
+                fluid_velocity.reshape(field_shape),
+                fluid_mass,
+                positions.transpose(1, 0, 2),
+                velocities.transpose(1, 0, 2),
+                relax_rates,
+                bin_element.reshape(1, bins),
+                bin_fill.reshape(1, bins),
+            )
+        )
     )
     for turn in range(PASSES):
         last = turn == PASSES - 1
@@ -391,7 +453,7 @@
             compiler_params=params,
             name="advance",
         )(q, viscosity, axial_speed, *halos)
-    return (q.reshape(3, NODES, sec_cells, air_cells), particles_out)
+    return (q.reshape(3, NODES, sec_cells, air_cells), particles_out.transpose(1, 0, 2))
 
 
 def solution(mesh):

time: 130 us -> 85 us (0.65)
  Pallas kernels: 68.1 us -> 45.5 us
  starting transfers between devices: 50.3 us -> 32.1 us
  local copies, waits for them, and re-layouts: 7.02 us -> 0.01 us
  waiting for transfers between devices: 2.2 us -> 5.98 us
    pallas_call x1, Pallas kernels: 61.2 us -> 38.4 us  [local(): pl.pallas_call(particle_kernel, out_shape=(field, jax.ShapeDtypeStruct((6...]
    ppermute x16, starting transfers between devices: 50.3 us -> 32.1 us  [swap(): return lax.ppermute(values, axis, pairs)]
    unnamed x17 -> x4, local copies, waits for them, and re-layouts: 7.02 us -> 0.01 us
    ppermute x16, waiting for transfers between devices: 2.2 us -> 5.98 us  [swap(): return lax.ppermute(values, axis, pairs)]
  transfers between devices with their start and end apart: 16 -> 16, of which waited for: 3 -> 4; matrix products, arithmetic and copies ran while one was open for 1% -> 0% of each run, Pallas kernels for 0% -> 0%
where the time goes in v1:
time: 85 us; the launch traced here: 84.3 us
  Pallas kernels  45.5 us (54%)
  starting transfers between devices  32.1 us (38%)
  waiting for transfers between devices  5.98 us (7%)
    pallas_call x1, Pallas kernels, local(): pl.pallas_call(particle_kernel, out_shape=(field, jax.ShapeDtypeStruct((6...  38.4 us
    ppermute x16, starting transfers between devices, swap(): return lax.ppermute(values, axis, pairs)  32.1 us
    pallas_call x4, Pallas kernels, local(): pl.pallas_call(functools.partial(pass_kernel, last), out_shape=(field,) +...  7.09 us
    ppermute x16, waiting for transfers between devices, swap(): return lax.ppermute(values, axis, pairs)  5.98 us
  transfers between devices with their start and end apart: 16, of which 4 were waited for; matrix products, arithmetic and copies ran while one was open for 0% of the time, Pallas kernels for 0%

profile of v1, /device:TPU:1, one launch (start us, length us, event | category | flops | bytes accessed | tf_op | source)
XLA Modules:
  0.0 84.3 jit_solution(7897188268851083342)
XLA Ops:
  0.6 0.0 copy-start.1
  0.6 0.0 copy-start
  0.7 38.4 %particles.1 = (f32[3,4,4,4,8,256]{5,4,3,2,1,0:T(8,128)S(1)}, f32[6,96,128]{2,1,0:T(8,128)}, f32[8,128]{1,0:T(8,128)S(1)}, f32[8,128]{1,0:T(8,128)S(1)}, f32[3,1...) custom-call(f32[3,4,4,4,8,256]{5,4,3,2,1,0:T(8,128)} %bitcast.7, f32[8,256]{1,0:T(8,128)} %mass_hbm.1, ...), custom_call_target="tpu_custom_call" | custom-call | tf_op jit(solution)/shard_map/particles/pallas_call | solution.py:408
  39.1 2.1 %collective-permute-start.2 = (f32[3,16,256]{2,1,0:T(8,128)S(1)}, f32[3,16,256]{2,1,0:T(8,128)S(1)}, u32[]{:S(2)}, u32[]{:S(2)}) collective-permute-start(f32[3,16,256]{2,1,0:T(8,128)S(1)} %get-tuple-element.26), channel_id=1, source_target_pairs={{0,1},{1,0},{2,3},{3,2},{4,5},{5,4},{6,7},{7,6},{8,9},{9,8},{10,11... | collective-permute-start | bytes 147464 | tf_op jit(solution)/shard_map/ppermute | solution.py:369
  41.1 0.7 collective-permute-start.3
  41.8 1.0 %collective-permute-start = (f32[8,128]{1,0:T(8,128)S(1)}, f32[8,128]{1,0:T(8,128)S(1)}, u32[]{:S(2)}, u32[]{:S(2)}) collective-permute-start(f32[8,128]{1,0:T(8,128)S(1)} %get-tuple-element.24), channel_id=1, source_target_pairs={{0,8},{8,0},{16,24},{24,16},{1,9},{9,1},{17,25},{25,17},{2,10},{10... | collective-permute-start | bytes 12296 | tf_op jit(solution)/shard_map/ppermute | solution.py:369
  42.8 3.0 %collective-permute-start.1 = (f32[8,128]{1,0:T(8,128)S(1)}, f32[8,128]{1,0:T(8,128)S(1)}, u32[]{:S(2)}, u32[]{:S(2)}) collective-permute-start(f32[8,128]{1,0:T(8,128)S(1)} %get-tuple-element.25), channel_id=1, source_target_pairs={{8,16},{16,8},{9,17},{17,9},{10,18},{18,10},{11,19},{19,11},{12,20... | collective-permute-start | bytes 12296 | tf_op jit(solution)/shard_map/ppermute | solution.py:369
  45.9 0.0 collective-permute-done.ha_first
  45.9 1.9 %collective-permute-done.1.ha_second = f32[8,128]{1,0:T(8,128)S(1)} collective-permute-done((f32[8,128]{1,0:T(8,128)S(1)}, f32[8,128]{1,0:T(8,128)S(1)}, u32[]{:S(2)}, u32[]{:S(2)}) %collective-permute-start.1) | collective-permute-done | bytes 4128 | tf_op jit(solution)/shard_map/ppermute | solution.py:369
  47.7 0.0 collective-permute-done.2.hs_first
  47.7 0.0 collective-permute-done.3.hs_second
  47.8 0.0 copy-done.1
  47.8 0.0 copy-done
  47.8 1.5 %advance.4 = (f32[3,4,4,4,8,256]{5,4,3,2,1,0:T(8,128)S(1)}, f32[8,128]{1,0:T(8,128)S(1)}, f32[8,128]{1,0:T(8,128)S(1)}, f32[3,16,256]{2,1,0:T(8,128)S(1)}, f32[3,16,256]{2,1,0:T(8,128)S(1)}) custom-call(f32[3,4,4,4,8,256]{5,4,3,2,1,0:T(8,128)S(1)} %get-tuple-element.23.q, f32[8,256]{1,0:T(8,128)S(1)} %copy-done, f32[8,256]{1,0:T(8,128)S(1)} %copy-done.1, ...), custom_call_target="tpu_custom_call" | custom-call | tf_op jit(solution)/shard_map/advance/pallas_call | solution.py:448
  49.3 4.1 %collective-permute-start.6 = (f32[3,16,256]{2,1,0:T(8,128)S(1)}, f32[3,16,256]{2,1,0:T(8,128)S(1)}, u32[]{:S(2)}, u32[]{:S(2)}) collective-permute-start(f32[3,16,256]{2,1,0:T(8,128)S(1)} %get-tuple-element.31), channel_id=1, source_target_pairs={{0,1},{1,0},{2,3},{3,2},{4,5},{5,4},{6,7},{7,6},{8,9},{9,8},{10,11... | collective-permute-start | bytes 147464 | tf_op jit(solution)/shard_map/ppermute | solution.py:369
  53.4 0.7 collective-permute-start.7
  54.0 0.1 collective-permute-start.4
  54.1 3.3 %collective-permute-start.5 = (f32[8,128]{1,0:T(8,128)S(1)}, f32[8,128]{1,0:T(8,128)S(1)}, u32[]{:S(2)}, u32[]{:S(2)}) collective-permute-start(f32[8,128]{1,0:T(8,128)S(1)} %get-tuple-element.30), channel_id=1, source_target_pairs={{8,16},{16,8},{9,17},{17,9},{10,18},{18,10},{11,19},{19,11},{12,20... | collective-permute-start | bytes 12296 | tf_op jit(solution)/shard_map/ppermute | solution.py:369
  57.5 0.0 collective-permute-done.4.ha_first
  57.5 1.6 %collective-permute-done.5.ha_second = f32[8,128]{1,0:T(8,128)S(1)} collective-permute-done((f32[8,128]{1,0:T(8,128)S(1)}, f32[8,128]{1,0:T(8,128)S(1)}, u32[]{:S(2)}, u32[]{:S(2)}) %collective-permute-start.5) | collective-permute-done | bytes 4128 | tf_op jit(solution)/shard_map/ppermute | solution.py:369
  59.0 0.0 collective-permute-done.6.hs_first
  59.0 0.0 collective-permute-done.7.hs_second
  59.1 1.5 %advance.5 = (f32[3,4,4,4,8,256]{5,4,3,2,1,0:T(8,128)S(1)}, f32[8,128]{1,0:T(8,128)S(1)}, f32[8,128]{1,0:T(8,128)S(1)}, f32[3,16,256]{2,1,0:T(8,128)S(1)}, f32[3,16,256]{2,1,0:T(8,128)S(1)}) custom-call(f32[3,4,4,4,8,256]{5,4,3,2,1,0:T(8,128)S(1)} %get-tuple-element.28.q, f32[8,256]{1,0:T(8,128)S(1)} %copy-done, f32[8,256]{1,0:T(8,128)S(1)} %copy-done.1, ...), custom_call_target="tpu_custom_call" | custom-call | tf_op jit(solution)/shard_map/advance/pallas_call | solution.py:448
  60.6 3.8 %collective-permute-start.10 = (f32[3,16,256]{2,1,0:T(8,128)S(1)}, f32[3,16,256]{2,1,0:T(8,128)S(1)}, u32[]{:S(2)}, u32[]{:S(2)}) collective-permute-start(f32[3,16,256]{2,1,0:T(8,128)S(1)} %get-tuple-element.36), channel_id=1, source_target_pairs={{0,1},{1,0},{2,3},{3,2},{4,5},{5,4},{6,7},{7,6},{8,9},{9,8},{10,11... | collective-permute-start | bytes 147464 | tf_op jit(solution)/shard_map/ppermute | solution.py:369
  64.4 0.7 collective-permute-start.11
  65.0 0.1 collective-permute-start.8
  65.1 3.9 %collective-permute-start.9 = (f32[8,128]{1,0:T(8,128)S(1)}, f32[8,128]{1,0:T(8,128)S(1)}, u32[]{:S(2)}, u32[]{:S(2)}) collective-permute-start(f32[8,128]{1,0:T(8,128)S(1)} %get-tuple-element.35), channel_id=1, source_target_pairs={{8,16},{16,8},{9,17},{17,9},{10,18},{18,10},{11,19},{19,11},{12,20... | collective-permute-start | bytes 12296 | tf_op jit(solution)/shard_map/ppermute | solution.py:369
  69.0 0.0 collective-permute-done.8.ha_first
  69.0 1.3 %collective-permute-done.9.ha_second = f32[8,128]{1,0:T(8,128)S(1)} collective-permute-done((f32[8,128]{1,0:T(8,128)S(1)}, f32[8,128]{1,0:T(8,128)S(1)}, u32[]{:S(2)}, u32[]{:S(2)}) %collective-permute-start.9) | collective-permute-done | bytes 4128 | tf_op jit(solution)/shard_map/ppermute | solution.py:369
  70.3 0.0 collective-permute-done.10.hs_first
  70.3 0.0 collective-permute-done.11.hs_second
  70.3 1.5 %advance.6 = (f32[3,4,4,4,8,256]{5,4,3,2,1,0:T(8,128)S(1)}, f32[8,128]{1,0:T(8,128)S(1)}, f32[8,128]{1,0:T(8,128)S(1)}, f32[3,16,256]{2,1,0:T(8,128)S(1)}, f32[3,16,256]{2,1,0:T(8,128)S(1)}) custom-call(f32[3,4,4,4,8,256]{5,4,3,2,1,0:T(8,128)S(1)} %get-tuple-element.33.q, f32[8,256]{1,0:T(8,128)S(1)} %copy-done, f32[8,256]{1,0:T(8,128)S(1)} %copy-done.1, ...), custom_call_target="tpu_custom_call" | custom-call | tf_op jit(solution)/shard_map/advance/pallas_call | solution.py:448
  71.8 4.1 %collective-permute-start.14 = (f32[3,16,256]{2,1,0:T(8,128)S(1)}, f32[3,16,256]{2,1,0:T(8,128)S(1)}, u32[]{:S(2)}, u32[]{:S(2)}) collective-permute-start(f32[3,16,256]{2,1,0:T(8,128)S(1)} %get-tuple-element.41), channel_id=1, source_target_pairs={{0,1},{1,0},{2,3},{3,2},{4,5},{5,4},{6,7},{7,6},{8,9},{9,8},{10,11... | collective-permute-start | bytes 147464 | tf_op jit(solution)/shard_map/ppermute | solution.py:369
  75.9 0.7 collective-permute-start.15
  76.5 0.1 collective-permute-start.12
  76.6 3.9 %collective-permute-start.13 = (f32[8,128]{1,0:T(8,128)S(1)}, f32[8,128]{1,0:T(8,128)S(1)}, u32[]{:S(2)}, u32[]{:S(2)}) collective-permute-start(f32[8,128]{1,0:T(8,128)S(1)} %get-tuple-element.40), channel_id=1, source_target_pairs={{8,16},{16,8},{9,17},{17,9},{10,18},{18,10},{11,19},{19,11},{12,20... | collective-permute-start | bytes 12296 | tf_op jit(solution)/shard_map/ppermute | solution.py:369
  80.5 0.0 collective-permute-done.12.ha_first
  80.6 1.3 %collective-permute-done.13.ha_second = f32[8,128]{1,0:T(8,128)S(1)} collective-permute-done((f32[8,128]{1,0:T(8,128)S(1)}, f32[8,128]{1,0:T(8,128)S(1)}, u32[]{:S(2)}, u32[]{:S(2)}) %collective-permute-start.13) | collective-permute-done | bytes 4128 | tf_op jit(solution)/shard_map/ppermute | solution.py:369
  81.8 0.0 collective-permute-done.14.hs_first
  81.8 0.0 collective-permute-done.15.hs_second
  81.8 2.5 %advance.7 = f32[3,4,4,4,8,256]{5,4,3,2,1,0:T(8,128)} custom-call(f32[3,4,4,4,8,256]{5,4,3,2,1,0:T(8,128)S(1)} %get-tuple-element.38.q, f32[8,256]{1,0:T(8,128)S(1)} %copy-done, f32[8,256]{1,0:T(8,128)S(1)} %copy-done.1, f32[8,128]{1,0:T(8,128)S(1)} %collective-permute-done.12.ha_first, f32[8,128]{1,0:T(8,128)S(1)} %collective-permute-done.13.ha_second, ...), custom_call_target="tpu_custom_call" | custom-call | tf_op jit(solution)/shard_map/advance/pallas_call | solution.py:448
Async XLA Ops:
  0.6 47.1 %copy-start.1 = (f32[8,256]{1,0:T(8,128)S(1)}, f32[8,256]{1,0:T(8,128)}, u32[]{:S(2)}) copy-start(f32[8,256]{1,0:T(8,128)} %speed.7) | copy-start | bytes 24580
  0.6 47.1 %copy-start = (f32[8,256]{1,0:T(8,128)S(1)}, f32[8,256]{1,0:T(8,128)}, u32[]{:S(2)}) copy-start(f32[8,256]{1,0:T(8,128)} %visc.7) | copy-start | bytes 24580
  39.1 8.7 %collective-permute-start.2 = (f32[3,16,256]{2,1,0:T(8,128)S(1)}, f32[3,16,256]{2,1,0:T(8,128)S(1)}, u32[]{:S(2)}, u32[]{:S(2)}) collective-permute-start(f32[3,16,256]{2,1,0:T(8,128)S(1)} %get-tuple-element.26), channel_id=1, source_target_pairs={{0,1},{1,0},{2,3},{3,2},{4,5},{5,4},{6,7},{7,6},{8,9},{9,8},{10,11... | collective-permute-start | bytes 147464 | tf_op jit(solution)/shard_map/ppermute | solution.py:369
  41.1 6.6 %collective-permute-start.3 = (f32[3,16,256]{2,1,0:T(8,128)S(1)}, f32[3,16,256]{2,1,0:T(8,128)S(1)}, u32[]{:S(2)}, u32[]{:S(2)}) collective-permute-start(f32[3,16,256]{2,1,0:T(8,128)S(1)} %get-tuple-element.27), channel_id=1, source_target_pairs={{1,2},{2,1},{3,4},{4,3},{5,6},{6,5},{9,10},{10,9},{11,12},{12,11},... | collective-permute-start | bytes 147464 | tf_op jit(solution)/shard_map/ppermute | solution.py:369
  41.8 4.1 %collective-permute-start = (f32[8,128]{1,0:T(8,128)S(1)}, f32[8,128]{1,0:T(8,128)S(1)}, u32[]{:S(2)}, u32[]{:S(2)}) collective-permute-start(f32[8,128]{1,0:T(8,128)S(1)} %get-tuple-element.24), channel_id=1, source_target_pairs={{0,8},{8,0},{16,24},{24,16},{1,9},{9,1},{17,25},{25,17},{2,10},{10... | collective-permute-start | bytes 12296 | tf_op jit(solution)/shard_map/ppermute | solution.py:369
  42.8 4.9 %collective-permute-start.1 = (f32[8,128]{1,0:T(8,128)S(1)}, f32[8,128]{1,0:T(8,128)S(1)}, u32[]{:S(2)}, u32[]{:S(2)}) collective-permute-start(f32[8,128]{1,0:T(8,128)S(1)} %get-tuple-element.25), channel_id=1, source_target_pairs={{8,16},{16,8},{9,17},{17,9},{10,18},{18,10},{11,19},{19,11},{12,20... | collective-permute-start | bytes 12296 | tf_op jit(solution)/shard_map/ppermute | solution.py:369
  49.3 9.7 %collective-permute-start.6 = (f32[3,16,256]{2,1,0:T(8,128)S(1)}, f32[3,16,256]{2,1,0:T(8,128)S(1)}, u32[]{:S(2)}, u32[]{:S(2)}) collective-permute-start(f32[3,16,256]{2,1,0:T(8,128)S(1)} %get-tuple-element.31), channel_id=1, source_target_pairs={{0,1},{1,0},{2,3},{3,2},{4,5},{5,4},{6,7},{7,6},{8,9},{9,8},{10,11... | collective-permute-start | bytes 147464 | tf_op jit(solution)/shard_map/ppermute | solution.py:369
  53.4 5.7 %collective-permute-start.7 = (f32[3,16,256]{2,1,0:T(8,128)S(1)}, f32[3,16,256]{2,1,0:T(8,128)S(1)}, u32[]{:S(2)}, u32[]{:S(2)}) collective-permute-start(f32[3,16,256]{2,1,0:T(8,128)S(1)} %get-tuple-element.32), channel_id=1, source_target_pairs={{1,2},{2,1},{3,4},{4,3},{5,6},{6,5},{9,10},{10,9},{11,12},{12,11},... | collective-permute-start | bytes 147464 | tf_op jit(solution)/shard_map/ppermute | solution.py:369
  54.0 3.4 %collective-permute-start.4 = (f32[8,128]{1,0:T(8,128)S(1)}, f32[8,128]{1,0:T(8,128)S(1)}, u32[]{:S(2)}, u32[]{:S(2)}) collective-permute-start(f32[8,128]{1,0:T(8,128)S(1)} %get-tuple-element.29), channel_id=1, source_target_pairs={{0,8},{8,0},{16,24},{24,16},{1,9},{9,1},{17,25},{25,17},{2,10},{10... | collective-permute-start | bytes 12296 | tf_op jit(solution)/shard_map/ppermute | solution.py:369
  54.1 4.9 %collective-permute-start.5 = (f32[8,128]{1,0:T(8,128)S(1)}, f32[8,128]{1,0:T(8,128)S(1)}, u32[]{:S(2)}, u32[]{:S(2)}) collective-permute-start(f32[8,128]{1,0:T(8,128)S(1)} %get-tuple-element.30), channel_id=1, source_target_pairs={{8,16},{16,8},{9,17},{17,9},{10,18},{18,10},{11,19},{19,11},{12,20... | collective-permute-start | bytes 12296 | tf_op jit(solution)/shard_map/ppermute | solution.py:369
  60.6 9.7 %collective-permute-start.10 = (f32[3,16,256]{2,1,0:T(8,128)S(1)}, f32[3,16,256]{2,1,0:T(8,128)S(1)}, u32[]{:S(2)}, u32[]{:S(2)}) collective-permute-start(f32[3,16,256]{2,1,0:T(8,128)S(1)} %get-tuple-element.36), channel_id=1, source_target_pairs={{0,1},{1,0},{2,3},{3,2},{4,5},{5,4},{6,7},{7,6},{8,9},{9,8},{10,11... | collective-permute-start | bytes 147464 | tf_op jit(solution)/shard_map/ppermute | solution.py:369
  64.4 5.9 %collective-permute-start.11 = (f32[3,16,256]{2,1,0:T(8,128)S(1)}, f32[3,16,256]{2,1,0:T(8,128)S(1)}, u32[]{:S(2)}, u32[]{:S(2)}) collective-permute-start(f32[3,16,256]{2,1,0:T(8,128)S(1)} %get-tuple-element.37), channel_id=1, source_target_pairs={{1,2},{2,1},{3,4},{4,3},{5,6},{6,5},{9,10},{10,9},{11,12},{12,11},... | collective-permute-start | bytes 147464 | tf_op jit(solution)/shard_map/ppermute | solution.py:369
  65.0 4.0 %collective-permute-start.8 = (f32[8,128]{1,0:T(8,128)S(1)}, f32[8,128]{1,0:T(8,128)S(1)}, u32[]{:S(2)}, u32[]{:S(2)}) collective-permute-start(f32[8,128]{1,0:T(8,128)S(1)} %get-tuple-element.34), channel_id=1, source_target_pairs={{0,8},{8,0},{16,24},{24,16},{1,9},{9,1},{17,25},{25,17},{2,10},{10... | collective-permute-start | bytes 12296 | tf_op jit(solution)/shard_map/ppermute | solution.py:369
  65.1 5.2 %collective-permute-start.9 = (f32[8,128]{1,0:T(8,128)S(1)}, f32[8,128]{1,0:T(8,128)S(1)}, u32[]{:S(2)}, u32[]{:S(2)}) collective-permute-start(f32[8,128]{1,0:T(8,128)S(1)} %get-tuple-element.35), channel_id=1, source_target_pairs={{8,16},{16,8},{9,17},{17,9},{10,18},{18,10},{11,19},{19,11},{12,20... | collective-permute-start | bytes 12296 | tf_op jit(solution)/shard_map/ppermute | solution.py:369
  71.8 10.0 %collective-permute-start.14 = (f32[3,16,256]{2,1,0:T(8,128)S(1)}, f32[3,16,256]{2,1,0:T(8,128)S(1)}, u32[]{:S(2)}, u32[]{:S(2)}) collective-permute-start(f32[3,16,256]{2,1,0:T(8,128)S(1)} %get-tuple-element.41), channel_id=1, source_target_pairs={{0,1},{1,0},{2,3},{3,2},{4,5},{5,4},{6,7},{7,6},{8,9},{9,8},{10,11... | collective-permute-start | bytes 147464 | tf_op jit(solution)/shard_map/ppermute | solution.py:369
  75.9 6.0 %collective-permute-start.15 = (f32[3,16,256]{2,1,0:T(8,128)S(1)}, f32[3,16,256]{2,1,0:T(8,128)S(1)}, u32[]{:S(2)}, u32[]{:S(2)}) collective-permute-start(f32[3,16,256]{2,1,0:T(8,128)S(1)} %get-tuple-element.42), channel_id=1, source_target_pairs={{1,2},{2,1},{3,4},{4,3},{5,6},{6,5},{9,10},{10,9},{11,12},{12,11},... | collective-permute-start | bytes 147464 | tf_op jit(solution)/shard_map/ppermute | solution.py:369
  76.5 4.0 %collective-permute-start.12 = (f32[8,128]{1,0:T(8,128)S(1)}, f32[8,128]{1,0:T(8,128)S(1)}, u32[]{:S(2)}, u32[]{:S(2)}) collective-permute-start(f32[8,128]{1,0:T(8,128)S(1)} %get-tuple-element.39), channel_id=1, source_target_pairs={{0,8},{8,0},{16,24},{24,16},{1,9},{9,1},{17,25},{25,17},{2,10},{10... | collective-permute-start | bytes 12296 | tf_op jit(solution)/shard_map/ppermute | solution.py:369
  76.6 5.2 %collective-permute-start.13 = (f32[8,128]{1,0:T(8,128)S(1)}, f32[8,128]{1,0:T(8,128)S(1)}, u32[]{:S(2)}, u32[]{:S(2)}) collective-permute-start(f32[8,128]{1,0:T(8,128)S(1)} %get-tuple-element.40), channel_id=1, source_target_pairs={{8,16},{16,8},{9,17},{17,9},{10,18},{18,10},{11,19},{19,11},{12,20... | collective-permute-start | bytes 12296 | tf_op jit(solution)/shard_map/ppermute | solution.py:369

commit v2 on v1

--- a/solution.py
+++ b/solution.py
@@ -53,31 +53,28 @@
     return lax.axis_index(axis) % 2 == 0
 
 
-def send_faces(q, sa_first, sa_second, ss_first, ss_second):
+def pack_columns(q, visc, speed, first, second):
     cells = q.shape[-1]
     lane = iota((SUB, LANE), 1)
-    nxt = jnp.zeros((SUB, LANE), f32)
-    prv = jnp.zeros((SUB, LANE), f32)
-    for comp in range(3):
-        for b in range(4):
-            for c in range(4):
-                i = comp * 16 + b * 4 + c
-                tail = q[comp, 3, b, c, :, cells - LANE :]
-                head = q[comp, 0, b, c, :, :LANE]
-                nxt = jnp.where(lane == i, pltpu.roll(tail, (i + 1) % LANE, 1), nxt)
-                prv = jnp.where(lane == i, pltpu.roll(head, i, 1), prv)
     even = is_even("airway")
-    sa_first[...] = jnp.where(even, nxt, prv)
-    sa_second[...] = jnp.where(even, prv, nxt)
-    even = is_even("section")
-    for comp in range(3):
-        for a in range(4):
-            for c in range(4):
-                i = a * 4 + c
-                tail = q[comp, a, 3, c, SUB - 1 : SUB, :]
-                head = q[comp, a, 0, c, 0:1, :]
-                ss_first[comp, i : i + 1, :] = jnp.where(even, tail, head)
-                ss_second[comp, i : i + 1, :] = jnp.where(even, head, tail)
+    for tile in range(9):
+        nxt = jnp.zeros((SUB, LANE), f32)
+        prv = jnp.zeros((SUB, LANE), f32)
+        for n in range(tile * 8, min(tile * 8 + 8, 66)):
+            for comp in range(3):
+                if n < NODES:
+                    tail = q[comp, n // 16, n // 4 % 4, n % 4, :, cells - LANE :]
+                    head = q[comp, n // 16, n // 4 % 4, n % 4, :, :LANE]
+                else:
+                    source = visc if n == NODES else speed
+                    tail = source[:, cells - LANE :]
+                    head = source[:, :LANE]
+                start = 64 * (n // 4 % 2) + 16 * comp + 4 * (n % 4)
+                here = (lane >= start) & (lane < start + 4)
+                nxt = jnp.where(here, pltpu.roll(tail, (start + 4) % LANE, 1), nxt)
+                prv = jnp.where(here, pltpu.roll(head, start, 1), prv)
+        first[tile] = jnp.where(even, nxt, prv)
+        second[tile] = jnp.where(even, prv, nxt)
 
 
 def second_line(q, v_even, v_odd):
@@ -87,94 +84,427 @@
     return [even - odd, even - third, even + third, even + odd]
 
 
-def pass_kernel(last, q, visc, speed, ha_first, ha_second, hs_first, hs_second, out, *sends):
-    cells = q.shape[-1]
-    tiles = cells // LANE
+def advance_tile(
+    load, store, v, g, beyond_next, beyond_prev, row_after, row_before, valid=None, drive=None
+):
     lane = iota((SUB, LANE), 1)
-    row = iota((SUB, LANE), 0)
-    is_last_lane = lane == LANE - 1
-    is_first_lane = lane == 0
-    is_last_row = row == SUB - 1
-    is_first_row = row == 0
+    v_even, v_odd = v * 1.125, v * 3.375
+    s_even, s_half = g * 1.125, g * 0.5
+    for b in range(4):
+        plane = [[load(a, b, c) for c in range(4)] for a in range(4)]
+        along_c = [second_line(plane[a], v_even, v_odd) for a in range(4)]
+        for c in range(4):
+            line = [plane[a][c] for a in range(4)]
+            rise = line[3] - line[0]
+            even = (line[0] + line[3]) - (line[1] + line[2])
+            odd = rise - 3.0 * (line[2] - line[1])
+            l_even = v_even * even
+            l_odd = v_odd * odd
+            l_third = l_odd * (1.0 / 3.0)
+            g_even = s_even * even
+            g_odd = s_even * odd
+            g_rise = s_half * rise
+            g_even3 = g_even * (1.0 / 3.0)
+            g_outer = g_rise + g_odd
+            g_inner = g_rise - g_odd * (1.0 / 3.0)
+            new = [
+                (l_even + g_even) - (l_odd + g_outer),
+                (l_even + g_even3) - (l_third + g_inner),
+                (l_even - g_even3) + (l_third - g_inner),
+                (l_even - g_even) + (l_odd - g_outer),
+            ]
+            new = [line[a] + (new[a] + along_c[a][c]) for a in range(4)]
+            after = pltpu.roll(line[0], LANE - 1, 1)
+            if beyond_next is not None:
+                after = jnp.where(lane == LANE - 1, pltpu.roll(beyond_next(0, b, c), LANE - 1, 1), after)
+            before = pltpu.roll(line[3], 1, 1)
+            if beyond_prev is not None:
+                before = jnp.where(lane == 0, pltpu.roll(beyond_prev(3, b, c), 1, 1), before)
+            new[3] = new[3] + penalty_weight * (after - line[3])
+            new[0] = new[0] + penalty_weight * (before - line[0])
+            for a in range(4):
+                store(a, b, c, new[a])
+    return v_even, v_odd
+
+
+def advance_rows(
+    load, partial, store, v, row_after, row_before, valid=None, drive=None
+):
+    v_even, v_odd = v * 1.125, v * 3.375
+    for a in range(4):
+        for c in range(4):
+            line = [load(a, b, c) for b in range(4)]
+            new = second_line(line, v_even, v_odd)
+            after = jnp.where(row_after, pltpu.roll(line[0], SUB - 1, 0), 0.0)
+            before = jnp.where(row_before, pltpu.roll(line[3], 1, 0), 0.0)
+            if drive is not None:
+                more_after, more_before = drive(a * 4 + c)
+                after = after + more_after
+                before = before + more_before
+            new[3] = new[3] + penalty_weight * (after - line[3])
+            new[0] = new[0] + penalty_weight * (before - line[0])
+            for b in range(4):
+                value = partial(a, b, c) + new[b]
+                store(a, b, c, value if valid is None else value * valid)
+
+
+def advance_main(source, target, visc, speed, row_after, row_before, drive=None):
+    tiles = source.shape[-1] // LANE
 
     def component(comp, carry):
-        forward = is_even("airway")
-        halo_after = jnp.where(forward, ha_first[...], ha_second[...])
-        halo_before = jnp.where(forward, ha_second[...], ha_first[...])
-        forward = is_even("section")
         for j in range(tiles):
             at = pl.ds(j * LANE, LANE)
-            v_even = visc[:, at] * 1.125
-            v_odd = visc[:, at] * 3.375
-            s_even = speed[:, at] * 1.125
-            s_odd = speed[:, at] * 1.125
-            s_half = speed[:, at] * 0.5
-            for b in range(4):
-                plane = [[q[comp, a, b, c, :, at] for c in range(4)] for a in range(4)]
-                along_c = [second_line(plane[a], v_even, v_odd) for a in range(4)]
-                for c in range(4):
-                    line = [plane[a][c] for a in range(4)]
-                    rise = line[3] - line[0]
-                    even = (line[0] + line[3]) - (line[1] + line[2])
-                    odd = rise - 3.0 * (line[2] - line[1])
-                    l_even = v_even * even
-                    l_odd = v_odd * odd
-                    l_third = l_odd * (1.0 / 3.0)
-                    g_even = s_even * even
-                    g_odd = s_odd * odd
-                    g_rise = s_half * rise
-                    g_even3 = g_even * (1.0 / 3.0)
-                    g_outer = g_rise + g_odd
-                    g_inner = g_rise - g_odd * (1.0 / 3.0)
-                    new = [
-                        (l_even + g_even) - (l_odd + g_outer),
-                        (l_even + g_even3) - (l_third + g_inner),
-                        (l_even - g_even3) + (l_third - g_inner),
-                        (l_even - g_even) + (l_odd - g_outer),
-                    ]
-                    new = [line[a] + (new[a] + along_c[a][c]) for a in range(4)]
-                    here = pltpu.roll(line[0], LANE - 1, 1)
-                    if j == tiles - 1:
-                        beyond = pltpu.roll(halo_after, (LANE - 1 - (comp * 16 + b * 4 + c)) % LANE, 1)
-                    else:
-                        beyond = pltpu.roll(q[comp, 0, b, c, :, pl.ds((j + 1) * LANE, LANE)], LANE - 1, 1)
-                    after = jnp.where(is_last_lane, beyond, here)
-                    here = pltpu.roll(line[3], 1, 1)
-                    if j == 0:
-                        beyond = pltpu.roll(halo_before, (LANE - (comp * 16 + b * 4 + c)) % LANE, 1)
-                    else:
-                        beyond = pltpu.roll(q[comp, 3, b, c, :, pl.ds((j - 1) * LANE, LANE)], 1, 1)
-                    before = jnp.where(is_first_lane, beyond, here)
-                    new[3] = new[3] + penalty_weight * (after - line[3])
-                    new[0] = new[0] + penalty_weight * (before - line[0])
-                    for a in range(4):
-                        out[comp, a, b, c, :, at] = new[a]
-            for a in range(4):
-                for c in range(4):
-                    line = [q[comp, a, b, c, :, at] for b in range(4)]
-                    new = second_line(line, v_even, v_odd)
-                    i = a * 4 + c
-                    first = jnp.broadcast_to(hs_first[comp, i : i + 1, at], (SUB, LANE))
-                    second = jnp.broadcast_to(hs_second[comp, i : i + 1, at], (SUB, LANE))
-                    after = jnp.where(
-                        is_last_row,
-                        jnp.where(forward, first, second),
-                        pltpu.roll(line[0], SUB - 1, 0),
+            at_next = pl.ds((j + 1) % tiles * LANE, LANE)
+            at_prev = pl.ds((j - 1) % tiles * LANE, LANE)
+
+            def load(a, b, c):
+                return source[comp, a, b, c, :, at]
+
+            def store(a, b, c, value):
+                target[comp, a, b, c, :, at] = value
+
+            v = visc[:, at]
+            advance_tile(
+                load,
+                store,
+                v,
+                speed[:, at],
+                lambda a, b, c: source[comp, a, b, c, :, at_next],
+                lambda a, b, c: source[comp, a, b, c, :, at_prev],
+                row_after,
+                row_before,
+            )
+            advance_rows(
+                load,
+                lambda a, b, c: target[comp, a, b, c, :, at],
+                store,
+                v,
+                row_after,
+                row_before,
+                drive=None if drive is None else functools.partial(drive, comp, at),
+            )
+        return carry
+
+    lax.fori_loop(0, 3, component, 0)
+
+
+def advance_strip(source, target, v, g, valid, row_after, row_before, drive=None):
+    def load(a, b, c):
+        return source[a, b, c]
+
+    def store(a, b, c, value):
+        target[a, b, c] = value
+
+    advance_tile(load, store, v, g, None, None, row_after, row_before)
+    advance_rows(
+        load,
+        lambda a, b, c: target[a, b, c],
+        store,
+        v,
+        row_after,
+        row_before,
+        valid=valid,
+        drive=drive,
+    )
+
+
+FACE_BLOCKS = PASSES * 3 * 2
+STRIP_BLOCKS = PASSES
+COEFFICIENTS = FACE_BLOCKS + STRIP_BLOCKS
+
+
+def face_row(faces, turn, comp, i, at):
+    return faces[(turn * 3 + comp) * 2 + i // SUB, i % SUB : i % SUB + 1, at]
+
+
+def strip_at(turn, i):
+    block = FACE_BLOCKS + turn // 2 * 2 + i // SUB
+    return block, i % SUB, pl.ds(turn % 2 * LANE, LANE)
+
+
+def block_rows():
+    row = iota((SUB, LANE), 0)
+    return row != SUB - 1, row != 0
+
+
+def strip_valid():
+    lane = iota((SUB, LANE), 1)
+    place = lane % 16
+    index = lax.axis_index("airway")
+    first = (index == 0).astype(f32)
+    last = (index == lax.axis_size("airway") - 1).astype(f32)
+    left = ((lane < 64) & (place < 4)).astype(f32)
+    right = ((lane >= 64) & (place >= 8)).astype(f32)
+    return 1.0 - left * first - right * last
+
+
+def main_kernel(q, visc, speed, out, faces_first, faces_second, spare):
+    row_after, row_before = block_rows()
+    even = is_even("section")
+
+    def pack(source, turn):
+        for comp in range(3):
+            for i in range(16):
+                tail = source[comp, i // 4, 3, i % 4, SUB - 1 : SUB, :]
+                head = source[comp, i // 4, 0, i % 4, 0:1, :]
+                block = (turn * 3 + comp) * 2 + i // SUB
+                at = pl.ds(i % SUB, 1)
+                faces_first[block, at, :] = jnp.where(even, tail, head)
+                faces_second[block, at, :] = jnp.where(even, head, tail)
+
+    pack(q, 0)
+    advance_main(q, out, visc, speed, row_after, row_before)
+    pack(out, 1)
+    advance_main(out, spare, visc, speed, row_after, row_before)
+    pack(spare, 2)
+    advance_main(spare, out, visc, speed, row_after, row_before)
+    pack(out, 3)
+
+
+def strip_kernel(
+    q,
+    visc,
+    speed,
+    air_first,
+    air_second,
+    faces_first,
+    faces_second,
+    out,
+    strip_v,
+    strip_g,
+    sent_first,
+    sent_second,
+    spare,
+):
+    cells = q.shape[-1]
+    lane = iota((SUB, LANE), 1)
+    place = lane % 16
+    forward = is_even("airway")
+    left = (lane < 64) & (place < 4)
+    right = (lane >= 64) & (place >= 8)
+
+    def assemble(n, heads, tails):
+        total = jnp.zeros((SUB, LANE), f32)
+        for comp in range(3):
+            base = 16 * comp
+            total = jnp.where(lane // 16 == comp, pltpu.roll(heads[comp], base + 4, 1), total)
+            total = jnp.where(
+                lane // 16 == comp + 4, pltpu.roll(tails[comp], (base + 72) % LANE, 1), total
+            )
+        one = air_first[n // 8]
+        two = air_second[n // 8]
+        offset = 64 * (n // 4 % 2) + 4 * (n % 4)
+        from_next = jnp.where(forward, one, two)
+        from_prev = jnp.where(forward, two, one)
+        total = jnp.where(left, pltpu.roll(from_prev, (LANE - offset) % LANE, 1), total)
+        total = jnp.where(right, pltpu.roll(from_next, (LANE + 72 - offset) % LANE, 1), total)
+        return jnp.where(place < 12, total, 0.0)
+
+    for n in range(NODES):
+        a, b, c = n // 16, n // 4 % 4, n % 4
+        out[a, b, c] = assemble(
+            n,
+            [q[k, a, b, c, :, :LANE] for k in range(3)],
+            [q[k, a, b, c, :, cells - LANE :] for k in range(3)],
+        )
+    strip_v[...] = assemble(NODES, [visc[:, :LANE]] * 3, [visc[:, cells - LANE :]] * 3)
+    strip_g[...] = assemble(NODES + 1, [speed[:, :LANE]] * 3, [speed[:, cells - LANE :]] * 3)
+
+    row_after, row_before = block_rows()
+    even = is_even("section")
+    sent_first[:FACE_BLOCKS] = faces_first[...]
+    sent_second[:FACE_BLOCKS] = faces_second[...]
+
+    def send(block, row, at, tail, head):
+        sent_first[block, row : row + 1, at] = jnp.where(even, tail, head)
+        sent_second[block, row : row + 1, at] = jnp.where(even, head, tail)
+
+    def pack(source, turn):
+        for i in range(16):
+            block, row, at = strip_at(turn, i)
+            send(
+                block,
+                row,
+                at,
+                source[i // 4, 3, i % 4, SUB - 1 : SUB, :],
+                source[i // 4, 0, i % 4, 0:1, :],
+            )
+
+    everything = pl.ds(0, cells)
+    sent_first[COEFFICIENTS] = jnp.zeros((SUB, cells), f32)
+    sent_second[COEFFICIENTS] = jnp.zeros((SUB, cells), f32)
+    send(COEFFICIENTS, 0, everything, visc[SUB - 1 : SUB, :], visc[0:1, :])
+    send(COEFFICIENTS, 1, everything, speed[SUB - 1 : SUB, :], speed[0:1, :])
+    send(COEFFICIENTS, 2, pl.ds(0, LANE), strip_v[SUB - 1 : SUB, :], strip_v[0:1, :])
+    send(COEFFICIENTS, 2, pl.ds(LANE, LANE), strip_g[SUB - 1 : SUB, :], strip_g[0:1, :])
+
+    v, g, valid = strip_v[...], strip_g[...], strip_valid()
+    pack(out, 0)
+    advance_strip(out, spare, v, g, valid, row_after, row_before)
+    pack(spare, 1)
+    advance_strip(spare, out, v, g, valid, row_after, row_before)
+    pack(out, 2)
+    advance_strip(out, spare, v, g, valid, row_after, row_before)
+    pack(spare, 3)
+    out[...] = spare[...]
+
+
+def fourth_kernel(w, strip, visc, speed, strip_v, strip_g, w_out, strip_out):
+    row_after, row_before = block_rows()
+    advance_main(w, w_out, visc, speed, row_after, row_before)
+    advance_strip(
+        strip, strip_out, strip_v[...], strip_g[...], strip_valid(), row_after, row_before
+    )
+
+
+def edge_kernel(
+    w,
+    strip,
+    visc,
+    speed,
+    strip_v,
+    strip_g,
+    sent_first,
+    sent_second,
+    got_first,
+    got_second,
+    out,
+    e_one,
+    e_two,
+    z_one,
+    z_two,
+    e_visc,
+    e_speed,
+):
+    cells = w.shape[-1]
+    tiles = cells // LANE
+    row = iota((SUB, LANE), 0)
+    lane = iota((SUB, LANE), 1)
+    even = is_even("section")
+    index = lax.axis_index("section")
+    has_prev = index > 0
+    has_next = index < lax.axis_size("section") - 1
+    row_after = (row != SUB - 1) & ((row != 0) | has_prev)
+    row_before = (row != 0) & ((row != SUB - 1) | has_next)
+
+    def rows_of(own, prev_row, next_row):
+        moved = jnp.where(row == 1, pltpu.roll(own, 1, 0), 0.0)
+        moved = jnp.where(row == 2, pltpu.roll(own, 1, 0), moved)
+        moved = jnp.where((row == 5) | (row == 6), pltpu.roll(own, SUB - 1, 0), moved)
+        moved = jnp.where(row == 0, jnp.broadcast_to(prev_row, (SUB, LANE)), moved)
+        return jnp.where(row == SUB - 1, jnp.broadcast_to(next_row, (SUB, LANE)), moved)
+
+    def received(block, r, at):
+        one = got_first[block, r : r + 1, at]
+        two = got_second[block, r : r + 1, at]
+        return jnp.where(even, two, one), jnp.where(even, one, two)
+
+    for j in range(tiles):
+        at = pl.ds(j * LANE, LANE)
+        e_visc[:, at] = rows_of(visc[:, at], *received(COEFFICIENTS, 0, at))
+        e_speed[:, at] = rows_of(speed[:, at], *received(COEFFICIENTS, 1, at))
+    z_v = rows_of(strip_v[...], *received(COEFFICIENTS, 2, pl.ds(0, LANE)))
+    z_g = rows_of(strip_g[...], *received(COEFFICIENTS, 2, pl.ds(LANE, LANE)))
+    valid = strip_valid()
+
+    def forcing(pick):
+        one = jnp.broadcast_to(pick(got_first), (SUB, LANE))
+        two = jnp.broadcast_to(pick(got_second), (SUB, LANE))
+        own_one = jnp.broadcast_to(pick(sent_first), (SUB, LANE))
+        own_two = jnp.broadcast_to(pick(sent_second), (SUB, LANE))
+        from_next = jnp.where(even, one, two)
+        from_prev = jnp.where(even, two, one)
+        own_next = jnp.where(even, own_one, own_two)
+        own_prev = jnp.where(even, own_two, own_one)
+        after = jnp.where(
+            row == 6, from_next, jnp.where((row == 0) & has_prev, own_prev, 0.0)
+        )
+        before = jnp.where(
+            row == 1, from_prev, jnp.where((row == SUB - 1) & has_next, own_next, 0.0)
+        )
+        return after, before
+
+    def drive(turn, comp, at, i):
+        return forcing(lambda faces: face_row(faces, turn, comp, i, at))
+
+    def drive_strip(turn, i):
+        block, r, at = strip_at(turn, i)
+        return forcing(lambda faces: faces[block, r : r + 1, at])
+
+    def first_component(comp, carry):
+        for j in range(tiles):
+            at = pl.ds(j * LANE, LANE)
+            for i in range(16):
+                a, c = i // 4, i % 4
+                after, before = drive(0, comp, at, i)
+                e_one[comp, a, 3, c, :, at] = penalty_weight * after
+                e_one[comp, a, 0, c, :, at] = penalty_weight * before
+                for b in (1, 2):
+                    e_one[comp, a, b, c, :, at] = jnp.zeros((SUB, LANE), f32)
+        return carry
+
+    lax.fori_loop(0, 3, first_component, 0)
+    for i in range(16):
+        a, c = i // 4, i % 4
+        after, before = drive_strip(0, i)
+        z_one[a, 3, c] = penalty_weight * after * valid
+        z_one[a, 0, c] = penalty_weight * before * valid
+        for b in (1, 2):
+            z_one[a, b, c] = jnp.zeros((SUB, LANE), f32)
+
+    for turn, (source, target, z_source, z_target) in enumerate(
+        ((e_one, e_two, z_one, z_two), (e_two, e_one, z_two, z_one), (e_one, e_two, z_one, z_two)),
+        1,
+    ):
+        advance_main(
+            source,
+            target,
+            e_visc,
+            e_speed,
+            row_after,
+            row_before,
+            functools.partial(drive, turn),
+        )
+        advance_strip(
+            z_source,
+            z_target,
+            z_v,
+            z_g,
+            valid,
+            row_after,
+            row_before,
+            functools.partial(drive_strip, turn),
+        )
+
+    low = row < 2
+    high = row >= 6
+
+    def back(effect):
+        return jnp.where(
+            low, pltpu.roll(effect, SUB - 1, 0), jnp.where(high, pltpu.roll(effect, 1, 0), 0.0)
+        )
+
+    for n in range(NODES):
+        a, b, c = n // 16, n // 4 % 4, n % 4
+        z_one[a, b, c] = strip[a, b, c] + back(z_two[a, b, c])
+
+    def finish(comp, carry):
+        for n in range(NODES):
+            a, b, c = n // 16, n // 4 % 4, n % 4
+            edge = z_one[a, b, c]
+            for j in range(tiles):
+                at = pl.ds(j * LANE, LANE)
+                value = w[comp, a, b, c, :, at] + back(e_two[comp, a, b, c, :, at])
+                if j == 0:
+                    value = jnp.where(lane < 4, pltpu.roll(edge, LANE - 4 - 16 * comp, 1), value)
+                if j == tiles - 1:
+                    value = jnp.where(
+                        lane >= LANE - 4, pltpu.roll(edge, LANE - 4 - 68 - 16 * comp, 1), value
                     )
-                    before = jnp.where(
-                        is_first_row,
-                        jnp.where(forward, second, first),
-                        pltpu.roll(line[3], 1, 0),
-                    )
-                    new[3] = new[3] + penalty_weight * (after - line[3])
-                    new[0] = new[0] + penalty_weight * (before - line[0])
-                    for b in range(4):
-                        out[comp, a, b, c, :, at] = out[comp, a, b, c, :, at] + new[b]
+                out[comp, a, b, c, :, at] = value
         return carry
 
-    lax.fori_loop(0, 3, component, 0)
-    if not last:
-        send_faces(out, *sends)
+    lax.fori_loop(0, 3, finish, 0)
 
 
 def particle_kernel(
@@ -185,12 +515,12 @@
     relax_hbm,
     element_hbm,
     fill_hbm,
+    visc_hbm,
+    speed_hbm,
     q_out,
     parts_out,
-    sa_first,
-    sa_second,
-    ss_first,
-    ss_second,
+    air_first,
+    air_second,
     rates,
     strides,
     occupied,
@@ -204,6 +534,8 @@
     relax,
     element_row,
     fill_row,
+    visc,
+    speed,
     arrived,
 ):
     copies = [
@@ -217,6 +549,8 @@
                 (positions, parts_out.at[0:3]),
                 (velocities, parts_out.at[3:6]),
                 (mass_hbm, mass),
+                (visc_hbm, visc),
+                (speed_hbm, speed),
             )
         )
     ]
@@ -358,7 +692,7 @@
         for comp in range(3):
             q_out[comp, a] = fluid[comp, a] - placed[1 + comp] * scale
 
-    send_faces(q_out, sa_first, sa_second, ss_first, ss_second)
+    pack_columns(q_out, visc, speed, air_first, air_second)
 
 
 def swap(values, axis, offset):
@@ -367,16 +701,6 @@
     for i in range(offset, count - 1, 2):
         pairs += [(i, i + 1), (i + 1, i)]
     return lax.ppermute(values, axis, pairs)
-
-
-def exchange(faces):
-    sa_first, sa_second, ss_first, ss_second = faces
-    return (
-        swap(sa_first, "airway", 0),
-        swap(sa_second, "airway", 1),
-        swap(ss_first, "section", 0),
-        swap(ss_second, "section", 1),
-    )
 
 
 def local(
@@ -396,20 +720,19 @@
     lanes_bins = -(-bins // LANE) * LANE
     field_shape = (3, 4, 4, 4, sec_cells, air_cells)
     field = jax.ShapeDtypeStruct(field_shape, f32)
-    face_shapes = (
-        jax.ShapeDtypeStruct((sec_cells, LANE), f32),
-        jax.ShapeDtypeStruct((sec_cells, LANE), f32),
-        jax.ShapeDtypeStruct((3, 16, air_cells), f32),
-        jax.ShapeDtypeStruct((3, 16, air_cells), f32),
-    )
+    air_shape = jax.ShapeDtypeStruct((9, SUB, LANE), f32)
+    strip_shape = jax.ShapeDtypeStruct((4, 4, 4, SUB, LANE), f32)
+    tile_shape = jax.ShapeDtypeStruct((SUB, LANE), f32)
+    face_shape = jax.ShapeDtypeStruct((FACE_BLOCKS, SUB, air_cells), f32)
+    sent_shape = jax.ShapeDtypeStruct((COEFFICIENTS + 1, SUB, air_cells), f32)
     vmem = pl.BlockSpec(memory_space=pltpu.VMEM)
     hbm = pl.BlockSpec(memory_space=pltpu.HBM)
     params = pltpu.CompilerParams(vmem_limit_bytes=48 * 1024 * 1024)
-    q, particles_out, *faces = pl.pallas_call(
+    q, particles_out, air_first, air_second = pl.pallas_call(
         particle_kernel,
-        out_shape=(field, jax.ShapeDtypeStruct((6, bins, LANE), f32)) + face_shapes,
-        in_specs=[hbm] * 7,
-        out_specs=(vmem,) * 6,
+        out_shape=(field, jax.ShapeDtypeStruct((6, bins, LANE), f32), air_shape, air_shape),
+        in_specs=[hbm] * 9,
+        out_specs=(vmem,) * 4,
         scratch_shapes=[
             pltpu.VMEM((bins, LANE), f32),
             pltpu.VMEM((bins, LANE), f32),
@@ -424,7 +747,9 @@
             pltpu.VMEM(relax_rates.shape, f32),
             pltpu.VMEM((1, bins), jnp.int32),
             pltpu.VMEM((1, bins), jnp.int32),
-            pltpu.SemaphoreType.DMA((7,)),
+            pltpu.VMEM(viscosity.shape, f32),
+            pltpu.VMEM(axial_speed.shape, f32),
+            pltpu.SemaphoreType.DMA((9,)),
         ],
         compiler_params=params,
         name="particles",
@@ -439,20 +764,69 @@
                 relax_rates,
                 bin_element.reshape(1, bins),
                 bin_fill.reshape(1, bins),
+                viscosity,
+                axial_speed,
             )
         )
     )
-    for turn in range(PASSES):
-        last = turn == PASSES - 1
-        halos = exchange(faces)
-        q, *faces = pl.pallas_call(
-            functools.partial(pass_kernel, last),
-            out_shape=(field,) + (() if last else face_shapes),
-            in_specs=[vmem] * 7,
-            out_specs=(vmem,) * (1 if last else 5),
+
+    def call(kernel, name, outputs, scratch, *operands):
+        return pl.pallas_call(
+            kernel,
+            out_shape=outputs,
+            in_specs=[vmem] * len(operands),
+            out_specs=jax.tree.map(lambda _: vmem, outputs),
+            scratch_shapes=[pltpu.VMEM(shape.shape, f32) for shape in scratch],
             compiler_params=params,
-            name="advance",
-        )(q, viscosity, axial_speed, *halos)
+            cost_estimate=pl.CostEstimate(
+                flops=30 * fluid_velocity.size, bytes_accessed=8 * fluid_velocity.size, transcendentals=0
+            ),
+            name=name,
+        )(*operands)
+
+    got_air = (swap(air_first, "airway", 0), swap(air_second, "airway", 1))
+    w, *faces = call(
+        main_kernel, "main", (field, face_shape, face_shape), (field,), q, viscosity, axial_speed
+    )
+    strip, strip_v, strip_g, *sent = call(
+        strip_kernel,
+        "strip",
+        (strip_shape, tile_shape, tile_shape, sent_shape, sent_shape),
+        (strip_shape,),
+        q,
+        viscosity,
+        axial_speed,
+        *got_air,
+        *faces,
+    )
+    got = (swap(sent[0], "section", 0), swap(sent[1], "section", 1))
+    w, strip = call(
+        fourth_kernel,
+        "fourth",
+        (field, strip_shape),
+        (),
+        w,
+        strip,
+        viscosity,
+        axial_speed,
+        strip_v,
+        strip_g,
+    )
+    mass_tile = jax.ShapeDtypeStruct(fluid_mass.shape, f32)
+    q = call(
+        edge_kernel,
+        "edge",
+        field,
+        (field, field, strip_shape, strip_shape, mass_tile, mass_tile),
+        w,
+        strip,
+        viscosity,
+        axial_speed,
+        strip_v,
+        strip_g,
+        *sent,
+        *got,
+    )
     return (q.reshape(3, NODES, sec_cells, air_cells), particles_out.transpose(1, 0, 2))
 
 

time: 85 us -> 66.5 us (0.78)
  starting transfers between devices: 32.1 us -> 6.73 us
  Pallas kernels: 45.5 us -> 52.2 us
    ppermute x16 -> x4, starting transfers between devices: 32.1 us -> 6.73 us  [swap(): return lax.ppermute(values, axis, pairs)]
    pallas_call x4, Pallas kernels: 7.09 us -> 13.6 us  [call(): pl.pallas_call(kernel, out_shape=outputs, in_specs=[vmem] * len(operands)...]
    ppermute x16 -> x4, waiting for transfers between devices: 5.98 us -> 6.64 us  [swap(): return lax.ppermute(values, axis, pairs)]
  transfers between devices with their start and end apart: 16 -> 4, of which waited for: 4 -> 1; matrix products, arithmetic and copies ran while one was open for 0% -> 0% of each run, Pallas kernels for 0% -> 8%
where the time goes in v2:
time: 66.5 us; the launch traced here: 66.3 us
  Pallas kernels  52.2 us (78%)
  starting transfers between devices  6.73 us (10%)
  waiting for transfers between devices  6.64 us (10%)
  between operations  0.72 us (1%)
    pallas_call x1, Pallas kernels, local(): pl.pallas_call(particle_kernel, out_shape=(field, jax.ShapeDtypeStruct((6...  38.7 us
    pallas_call x4, Pallas kernels, call(): pl.pallas_call(kernel, out_shape=outputs, in_specs=[vmem] * len(operands)...  13.6 us
    ppermute x4, starting transfers between devices, swap(): return lax.ppermute(values, axis, pairs)  6.73 us
    ppermute x4, waiting for transfers between devices, swap(): return lax.ppermute(values, axis, pairs)  6.64 us
  transfers between devices with their start and end apart: 4, of which 1 were waited for; matrix products, arithmetic and copies ran while one was open for 0% of the time, Pallas kernels for 8%

profile of v2, /device:TPU:1, one launch (start us, length us, event | category | flops | bytes accessed | tf_op | source)
XLA Modules:
  0.0 66.3 jit_solution(14624317234167626380)
XLA Ops:
  0.6 0.0 copy-start.1
  0.6 0.0 copy-start
  0.7 38.7 %particles.1 = (f32[3,4,4,4,8,256]{5,4,3,2,1,0:T(8,128)S(1)}, f32[6,96,128]{2,1,0:T(8,128)}, f32[9,8,128]{2,1,0:T(8,128)S(1)}, f32[9,8,128]{2,1,0:T(8,128)S(1)}) custom-call(f32[3,4,4,4,8,256]{5,4,3,2,1,0:T(8,128)} %bitcast.7, f32[8,256]{1,0:T(8,128)} %mass_hbm.1, f32[3,96,128]{2,1,0:T(8,128)} %bitcast.9, f32[3,96,128]{2,1,0:T(8,128)} %bitcast.10, ...), custom_call_target="tpu_custom_call" | custom-call | tf_op jit(solution)/shard_map/particles/pallas_call | solution.py:731
  39.3 0.1 collective-permute-start
  39.4 4.7 %collective-permute-start.1 = (f32[9,8,128]{2,1,0:T(8,128)S(1)}, f32[9,8,128]{2,1,0:T(8,128)S(1)}, u32[]{:S(2)}, u32[]{:S(2)}) collective-permute-start(f32[9,8,128]{2,1,0:T(8,128)S(1)} %get-tuple-element.19), channel_id=1, source_target_pairs={{8,16},{16,8},{9,17},{17,9},{10,18},{18,10},{11,19},{19,11},{12,20... | collective-permute-start | bytes 110600 | tf_op jit(solution)/shard_map/ppermute | solution.py:703
  44.1 0.0 copy-done.1
  44.1 0.0 copy-done
  44.1 3.9 %main.1 = (f32[3,4,4,4,8,256]{5,4,3,2,1,0:T(8,128)S(1)}, f32[24,8,256]{2,1,0:T(8,128)S(1)}, f32[24,8,256]{2,1,0:T(8,128)S(1)}) custom-call(f32[3,4,4,4,8,256]{5,4,3,2,1,0:T(8,128)S(1)} %get-tuple-element.16.q, f32[8,256]{1,0:T(8,128)S(1)} %copy-done, f32[8,256]{1,0:T(8,128)S(1)} %copy-done.1), custom_call_target="tpu_custom_call" | custom-call | flops 11796480 | bytes 3145728 | tf_op jit(solution)/shard_map/main/pallas_call | solution.py:774
  48.1 0.0 collective-permute-done.air_first
  48.1 0.0 collective-permute-done.1.air_second
  48.1 1.3 %strip.1 = (f32[4,4,4,8,128]{4,3,2,1,0:T(8,128)S(1)}, f32[8,128]{1,0:T(8,128)S(1)}, f32[8,128]{1,0:T(8,128)S(1)}, f32[29,8,256]{2,1,0:T(8,128)S(1)}, f32[29,8,256]{2,1,0:T(8,128)S(1)}) custom-call(f32[3,4,4,4,8,256]{5,4,3,2,1,0:T(8,128)S(1)} %get-tuple-element.16.q, f32[8,256]{1,0:T(8,128)S(1)} %copy-done, f32[8,256]{1,0:T(8,128)S(1)} %copy-done.1, ...), custom_call_target="tpu_custom_call" | custom-call | flops 11796480 | bytes 3145728 | tf_op jit(solution)/shard_map/strip/pallas_call | solution.py:774
  49.4 1.3 %collective-permute-start.2 = (f32[29,8,256]{2,1,0:T(8,128)S(1)}, f32[29,8,256]{2,1,0:T(8,128)S(1)}, u32[]{:S(2)}, u32[]{:S(2)}) collective-permute-start(f32[29,8,256]{2,1,0:T(8,128)S(1)} %get-tuple-element.27.sent_first), channel_id=1, source_target_pairs={{0,1},{1,0},{2,3},{3,2},{4,5},{5,4},{6,7},{7,6},{8,9},{9,8},{10,11... | collective-permute-start | bytes 712712 | tf_op jit(solution)/shard_map/ppermute | solution.py:703
  50.7 0.7 %collective-permute-start.3 = (f32[29,8,256]{2,1,0:T(8,128)S(1)}, f32[29,8,256]{2,1,0:T(8,128)S(1)}, u32[]{:S(2)}, u32[]{:S(2)}) collective-permute-start(f32[29,8,256]{2,1,0:T(8,128)S(1)} %get-tuple-element.28.sent_second), channel_id=1, source_target_pairs={{1,2},{2,1},{3,4},{4,3},{5,6},{6,5},{9,10},{10,9},{11,12},{12,11},... | collective-permute-start | bytes 712712 | tf_op jit(solution)/shard_map/ppermute | solution.py:703
  51.3 1.5 %fourth.1 = (f32[3,4,4,4,8,256]{5,4,3,2,1,0:T(8,128)S(1)}, f32[4,4,4,8,128]{4,3,2,1,0:T(8,128)S(1)}) custom-call(f32[3,4,4,4,8,256]{5,4,3,2,1,0:T(8,128)S(1)} %get-tuple-element.17.w, f32[4,4,4,8,128]{4,3,2,1,0:T(8,128)S(1)} %get-tuple-element.22.strip, f32[8,256]{1,0:T(8,128)S(1)} %copy-done, f32[8,256]{1,0:T(8,128)S(1)} %copy-done.1, ...), custom_call_target="tpu_custom_call" | custom-call | flops 11796480 | bytes 3145728 | tf_op jit(solution)/shard_map/fourth/pallas_call | solution.py:774
  52.8 6.6 %collective-permute-done.2.got_first = f32[29,8,256]{2,1,0:T(8,128)S(1)} collective-permute-done((f32[29,8,256]{2,1,0:T(8,128)S(1)}, f32[29,8,256]{2,1,0:T(8,128)S(1)}, u32[]{:S(2)}, u32[]{:S(2)}) %collective-permute-start.2) | collective-permute-done | bytes 237600 | tf_op jit(solution)/shard_map/ppermute | solution.py:703
  59.4 0.0 collective-permute-done.3.got_second
  59.4 6.9 %edge.1 = f32[3,4,4,4,8,256]{5,4,3,2,1,0:T(8,128)} custom-call(f32[3,4,4,4,8,256]{5,4,3,2,1,0:T(8,128)S(1)} %get-tuple-element.25.w, f32[4,4,4,8,128]{4,3,2,1,0:T(8,128)S(1)} %get-tuple-element.26.strip, f32[8,256]{1,0:T(8,128)S(1)} %copy-done, f32[8,256]{1,0:T(8,128)S(1)} %copy-done.1, f32[8,128]{1,0:T(8,128)S(1)} %get-tuple-element.23.strip_v, ...), custom_call_target="tpu_custom_call" | custom-call | flops 11796480 | bytes 3145728 | tf_op jit(solution)/shard_map/edge/pallas_call | solution.py:774
Async XLA Ops:
  0.6 43.5 %copy-start.1 = (f32[8,256]{1,0:T(8,128)S(1)}, f32[8,256]{1,0:T(8,128)}, u32[]{:S(2)}) copy-start(f32[8,256]{1,0:T(8,128)} %speed.7) | copy-start | bytes 24580
  0.6 43.5 %copy-start = (f32[8,256]{1,0:T(8,128)S(1)}, f32[8,256]{1,0:T(8,128)}, u32[]{:S(2)}) copy-start(f32[8,256]{1,0:T(8,128)} %visc.7) | copy-start | bytes 24580
  39.3 8.8 %collective-permute-start = (f32[9,8,128]{2,1,0:T(8,128)S(1)}, f32[9,8,128]{2,1,0:T(8,128)S(1)}, u32[]{:S(2)}, u32[]{:S(2)}) collective-permute-start(f32[9,8,128]{2,1,0:T(8,128)S(1)} %get-tuple-element.18), channel_id=1, source_target_pairs={{0,8},{8,0},{16,24},{24,16},{1,9},{9,1},{17,25},{25,17},{2,10},{10... | collective-permute-start | bytes 110600 | tf_op jit(solution)/shard_map/ppermute | solution.py:703
  39.4 8.7 %collective-permute-start.1 = (f32[9,8,128]{2,1,0:T(8,128)S(1)}, f32[9,8,128]{2,1,0:T(8,128)S(1)}, u32[]{:S(2)}, u32[]{:S(2)}) collective-permute-start(f32[9,8,128]{2,1,0:T(8,128)S(1)} %get-tuple-element.19), channel_id=1, source_target_pairs={{8,16},{16,8},{9,17},{17,9},{10,18},{18,10},{11,19},{19,11},{12,20... | collective-permute-start | bytes 110600 | tf_op jit(solution)/shard_map/ppermute | solution.py:703
  49.4 10.1 %collective-permute-start.2 = (f32[29,8,256]{2,1,0:T(8,128)S(1)}, f32[29,8,256]{2,1,0:T(8,128)S(1)}, u32[]{:S(2)}, u32[]{:S(2)}) collective-permute-start(f32[29,8,256]{2,1,0:T(8,128)S(1)} %get-tuple-element.27.sent_first), channel_id=1, source_target_pairs={{0,1},{1,0},{2,3},{3,2},{4,5},{5,4},{6,7},{7,6},{8,9},{9,8},{10,11... | collective-permute-start | bytes 712712 | tf_op jit(solution)/shard_map/ppermute | solution.py:703
  50.7 8.8 %collective-permute-start.3 = (f32[29,8,256]{2,1,0:T(8,128)S(1)}, f32[29,8,256]{2,1,0:T(8,128)S(1)}, u32[]{:S(2)}, u32[]{:S(2)}) collective-permute-start(f32[29,8,256]{2,1,0:T(8,128)S(1)} %get-tuple-element.28.sent_second), channel_id=1, source_target_pairs={{1,2},{2,1},{3,4},{4,3},{5,6},{6,5},{9,10},{10,9},{11,12},{12,11},... | collective-permute-start | bytes 712712 | tf_op jit(solution)/shard_map/ppermute | solution.py:703

commit v3 on v2

--- a/solution.py
+++ b/solution.py
@@ -13,7 +13,7 @@
 PASSES = 4
 SUB = 8
 LANE = 128
-GROUPS_TOGETHER = 4
+GROUPS_TOGETHER = 6
 
 penalty_weight = 0.25
 stride_step = 0.05
@@ -525,7 +525,8 @@
     strides,
     occupied,
     nodal,
-    sums,
+    sums_even,
+    sums_odd,
     totals,
     one_hot,
     rows_ref,
@@ -578,7 +579,6 @@
     lane_bins = iota((SUB, lanes_bins), 1)
     row_bins = iota((SUB, lanes_bins), 0)
     one_hot[...] = jnp.zeros(one_hot.shape, bf16)
-    section_cols = []
     for g in range(groups):
         own = lane_bins == row_bins + g * SUB
         element = jnp.sum(jnp.where(own, element_lanes, 0.0), axis=1, keepdims=True)
@@ -586,7 +586,6 @@
         section = jnp.zeros_like(element)
         for s in range(1, SUB):
             section = section + (element >= float(s * cells)).astype(f32)
-        section_cols.append(section)
         column = element - section * float(cells)
         at = pl.ds(g * SUB, SUB)
         occ = (lane8.astype(f32) < fill).astype(f32)
@@ -598,26 +597,49 @@
     copies[2].wait()
 
     spread = (iota((LANE, LANE), 0) // SUB == iota((LANE, LANE), 1) // SUB).astype(bf16)
-    section_col = jnp.concatenate(section_cols, axis=0)
-    in_section = (iota((bins, LANE), 1) % SUB).astype(f32) == section_col
-    hot_bins = one_hot[:bins, :]
+    in_section_rows = (iota((LANE, lanes_bins), 0) % SUB).astype(f32) == section_lanes
+    hot_all = one_hot[...]
+    sources = []
     for comp in range(3):
         for a in range(4):
-            i = comp * 4 + a
-            values = fluid[comp, a].reshape(16 * SUB, cells)
-            for part, source in enumerate(split(values)):
-                picked = jnp.where(in_section, dot_t(hot_bins, source), 0.0).astype(bf16)
-                wide = dot(picked, spread)
-                for g in range(groups):
-                    block = wide[g * SUB : (g + 1) * SUB, :] * same
-                    nodal[g, part * 96 + i * SUB : part * 96 + (i + 1) * SUB, :] = block.astype(bf16)
+            sources += split(fluid[comp, a].reshape(16 * SUB, cells))
+    found = dot_t(jnp.concatenate(sources, axis=0), hot_all)
+    picked = [
+        jnp.where(in_section_rows, found[k * LANE : (k + 1) * LANE], 0.0).T.astype(bf16)
+        for k in range(24)
+    ]
+    wide = dot(jnp.concatenate(picked, axis=0), spread)
+    for i in range(12):
+        for part in range(2):
+            rows = wide[(i * 2 + part) * lanes_bins : (i * 2 + part + 1) * lanes_bins]
+            for g in range(groups):
+                block = rows[g * SUB : (g + 1) * SUB, :] * same
+                start = part * 96 + i * SUB
+                nodal[g, start : start + SUB, :] = block.astype(bf16)
 
     for copy in copies[3:]:
         copy.wait()
     rates[...] = relax[...] * occupied[...]
     totals[...] = jnp.zeros(totals.shape, f32)
 
+    sums = (sums_even, sums_odd)
+
+    def sum_lanes(first, turn):
+        buffer = sums[first // GROUPS_TOGETHER % 2]
+        for slot in range(GROUPS_TOGETHER):
+            at = pl.ds((first + slot) * SUB, SUB)
+            total = totals[turn // 8, at, :]
+            for n in range(16):
+                j = turn * 16 + n
+                over_lanes = jnp.sum(buffer[slot, j], axis=1, keepdims=True)
+                total = jnp.where(lane8 == j % LANE, over_lanes, total)
+                buffer[slot, j] = jnp.zeros((SUB, LANE), f32)
+            totals[turn // 8, at, :] = total
+
     def substep(first, turn, carry):
+        if first:
+            sum_lanes(first - GROUPS_TOGETHER, turn)
+        buffer = sums[first // GROUPS_TOGETHER % 2]
         for slot in range(GROUPS_TOGETHER):
             g = first + slot
             at = pl.ds(g * SUB, SUB)
@@ -644,38 +666,23 @@
             for n in range(16):
                 for i in range(12):
                     j = i * 16 + n
-                    sums[slot, j] = sums[slot, j] + across[n] * pushes[i]
+                    buffer[slot, j] = buffer[slot, j] + across[n] * pushes[i]
             for n in range(16):
                 square = across[n] * across[n]
                 for a in range(4):
                     j = (12 + a) * 16 + n
-                    sums[slot, j] = sums[slot, j] + square * weighs[a]
+                    buffer[slot, j] = buffer[slot, j] + square * weighs[a]
         return carry
 
-    def over_lanes(slot, start):
-        terms = [sums[slot, start + n] for n in range(LANE)]
-        width = 1
-        while width < LANE:
-            upper = (lane8 // width) % 2 == 1
-            terms = [
-                jnp.where(upper, odd, even) + pltpu.roll(jnp.where(upper, even, odd), width, 1)
-                for even, odd in zip(terms[0::2], terms[1::2])
-            ]
-            width *= 2
-        return terms[0]
-
+    for buffer in sums:
+        buffer[...] = jnp.zeros(buffer.shape, f32)
     for first in range(0, groups, GROUPS_TOGETHER):
-        sums[...] = jnp.zeros(sums.shape, f32)
         lax.fori_loop(0, SUBSTEPS, functools.partial(substep, first), 0)
-        for slot in range(GROUPS_TOGETHER):
-            at = pl.ds((first + slot) * SUB, SUB)
-            totals[at, :LANE] = over_lanes(slot, 0)
-            totals[at, LANE:] = over_lanes(slot, LANE)
-
-    in_section_rows = (iota((LANE, lanes_bins), 0) % SUB).astype(f32) == section_lanes
-    hot_all = one_hot[...]
+    for turn in range(16):
+        sum_lanes(groups - GROUPS_TOGETHER, turn)
+
     spread_rows = (iota((LANE, 16), 0) // SUB == iota((LANE, 16), 1)).astype(bf16)
-    by_node = jnp.concatenate([totals[:, :LANE].T, totals[:, LANE:].T], axis=0)
+    by_node = jnp.concatenate([totals[0].T, totals[1].T], axis=0)
 
     for a in range(4):
         highs = []
@@ -739,7 +746,8 @@
             pltpu.VMEM((bins, LANE), f32),
             pltpu.VMEM((groups, 192, LANE), bf16),
             pltpu.VMEM((GROUPS_TOGETHER, 256, SUB, LANE), f32),
-            pltpu.VMEM((lanes_bins, 256), f32),
+            pltpu.VMEM((GROUPS_TOGETHER, 256, SUB, LANE), f32),
+            pltpu.VMEM((2, lanes_bins, LANE), f32),
             pltpu.VMEM((lanes_bins, air_cells), bf16),
             pltpu.VMEM((SUB, lanes_bins), f32),
             pltpu.VMEM(field_shape, f32),

time: 66.5 us -> 57.8 us (0.87)
  Pallas kernels: 52.2 us -> 43.7 us
    pallas_call x1, Pallas kernels: 38.7 us -> 30.2 us  [local(): pl.pallas_call(particle_kernel, out_shape=(field, jax.ShapeDtypeStruct((6...]
  transfers between devices with their start and end apart: 4 -> 4, of which waited for: 1 -> 1; matrix products, arithmetic and copies ran while one was open for 0% -> 0% of each run, Pallas kernels for 8% -> 9%
where the time goes in v3:
time: 57.8 us; the launch traced here: 57.7 us
  Pallas kernels  43.7 us (76%)
  starting transfers between devices  6.73 us (12%)
  waiting for transfers between devices  6.46 us (11%)
  between operations  0.72 us (1%)
    pallas_call x1, Pallas kernels, local(): pl.pallas_call(particle_kernel, out_shape=(field, jax.ShapeDtypeStruct((6...  30.2 us
    pallas_call x4, Pallas kernels, call(): pl.pallas_call(kernel, out_shape=outputs, in_specs=[vmem] * len(operands)...  13.6 us
    ppermute x4, starting transfers between devices, swap(): return lax.ppermute(values, axis, pairs)  6.73 us
    ppermute x4, waiting for transfers between devices, swap(): return lax.ppermute(values, axis, pairs)  6.46 us
  transfers between devices with their start and end apart: 4, of which 1 were waited for; matrix products, arithmetic and copies ran while one was open for 0% of the time, Pallas kernels for 9%

profile of v3, /device:TPU:1, one launch (start us, length us, event | category | flops | bytes accessed | tf_op | source)
XLA Modules:
  0.0 57.7 jit_solution(13509732452431559602)
XLA Ops:
  0.6 0.0 copy-start.1
  0.6 0.0 copy-start
  0.7 30.2 %particles.1 = (f32[3,4,4,4,8,256]{5,4,3,2,1,0:T(8,128)S(1)}, f32[6,96,128]{2,1,0:T(8,128)}, f32[9,8,128]{2,1,0:T(8,128)S(1)}, f32[9,8,128]{2,1,0:T(8,128)S(1)}) custom-call(f32[3,4,4,4,8,256]{5,4,3,2,1,0:T(8,128)} %bitcast.7, f32[8,256]{1,0:T(8,128)} %mass_hbm.1, f32[3,96,128]{2,1,0:T(8,128)} %bitcast.9, f32[3,96,128]{2,1,0:T(8,128)} %bitcast.10, ...), custom_call_target="tpu_custom_call" | custom-call | tf_op jit(solution)/shard_map/particles/pallas_call | solution.py:738
  30.8 0.1 collective-permute-start
  30.9 4.5 %collective-permute-start.1 = (f32[9,8,128]{2,1,0:T(8,128)S(1)}, f32[9,8,128]{2,1,0:T(8,128)S(1)}, u32[]{:S(2)}, u32[]{:S(2)}) collective-permute-start(f32[9,8,128]{2,1,0:T(8,128)S(1)} %get-tuple-element.19), channel_id=1, source_target_pairs={{8,16},{16,8},{9,17},{17,9},{10,18},{18,10},{11,19},{19,11},{12,20... | collective-permute-start | bytes 110600 | tf_op jit(solution)/shard_map/ppermute | solution.py:710
  35.5 0.0 copy-done.1
  35.5 0.0 copy-done
  35.5 3.9 %main.1 = (f32[3,4,4,4,8,256]{5,4,3,2,1,0:T(8,128)S(1)}, f32[24,8,256]{2,1,0:T(8,128)S(1)}, f32[24,8,256]{2,1,0:T(8,128)S(1)}) custom-call(f32[3,4,4,4,8,256]{5,4,3,2,1,0:T(8,128)S(1)} %get-tuple-element.16.q, f32[8,256]{1,0:T(8,128)S(1)} %copy-done, f32[8,256]{1,0:T(8,128)S(1)} %copy-done.1), custom_call_target="tpu_custom_call" | custom-call | flops 11796480 | bytes 3145728 | tf_op jit(solution)/shard_map/main/pallas_call | solution.py:782
  39.4 0.0 collective-permute-done.air_first
  39.4 0.0 collective-permute-done.1.air_second
  39.4 1.3 %strip.1 = (f32[4,4,4,8,128]{4,3,2,1,0:T(8,128)S(1)}, f32[8,128]{1,0:T(8,128)S(1)}, f32[8,128]{1,0:T(8,128)S(1)}, f32[29,8,256]{2,1,0:T(8,128)S(1)}, f32[29,8,256]{2,1,0:T(8,128)S(1)}) custom-call(f32[3,4,4,4,8,256]{5,4,3,2,1,0:T(8,128)S(1)} %get-tuple-element.16.q, f32[8,256]{1,0:T(8,128)S(1)} %copy-done, f32[8,256]{1,0:T(8,128)S(1)} %copy-done.1, ...), custom_call_target="tpu_custom_call" | custom-call | flops 11796480 | bytes 3145728 | tf_op jit(solution)/shard_map/strip/pallas_call | solution.py:782
  40.7 1.3 %collective-permute-start.2 = (f32[29,8,256]{2,1,0:T(8,128)S(1)}, f32[29,8,256]{2,1,0:T(8,128)S(1)}, u32[]{:S(2)}, u32[]{:S(2)}) collective-permute-start(f32[29,8,256]{2,1,0:T(8,128)S(1)} %get-tuple-element.27.sent_first), channel_id=1, source_target_pairs={{0,1},{1,0},{2,3},{3,2},{4,5},{5,4},{6,7},{7,6},{8,9},{9,8},{10,11... | collective-permute-start | bytes 712712 | tf_op jit(solution)/shard_map/ppermute | solution.py:710
  42.0 0.8 %collective-permute-start.3 = (f32[29,8,256]{2,1,0:T(8,128)S(1)}, f32[29,8,256]{2,1,0:T(8,128)S(1)}, u32[]{:S(2)}, u32[]{:S(2)}) collective-permute-start(f32[29,8,256]{2,1,0:T(8,128)S(1)} %get-tuple-element.28.sent_second), channel_id=1, source_target_pairs={{1,2},{2,1},{3,4},{4,3},{5,6},{6,5},{9,10},{10,9},{11,12},{12,11},... | collective-permute-start | bytes 712712 | tf_op jit(solution)/shard_map/ppermute | solution.py:710
  42.9 1.5 %fourth.1 = (f32[3,4,4,4,8,256]{5,4,3,2,1,0:T(8,128)S(1)}, f32[4,4,4,8,128]{4,3,2,1,0:T(8,128)S(1)}) custom-call(f32[3,4,4,4,8,256]{5,4,3,2,1,0:T(8,128)S(1)} %get-tuple-element.17.w, f32[4,4,4,8,128]{4,3,2,1,0:T(8,128)S(1)} %get-tuple-element.22.strip, f32[8,256]{1,0:T(8,128)S(1)} %copy-done, f32[8,256]{1,0:T(8,128)S(1)} %copy-done.1, ...), custom_call_target="tpu_custom_call" | custom-call | flops 11796480 | bytes 3145728 | tf_op jit(solution)/shard_map/fourth/pallas_call | solution.py:782
  44.3 6.5 %collective-permute-done.2.got_first = f32[29,8,256]{2,1,0:T(8,128)S(1)} collective-permute-done((f32[29,8,256]{2,1,0:T(8,128)S(1)}, f32[29,8,256]{2,1,0:T(8,128)S(1)}, u32[]{:S(2)}, u32[]{:S(2)}) %collective-permute-start.2) | collective-permute-done | bytes 237600 | tf_op jit(solution)/shard_map/ppermute | solution.py:710
  50.8 0.0 collective-permute-done.3.got_second
  50.8 6.9 %edge.1 = f32[3,4,4,4,8,256]{5,4,3,2,1,0:T(8,128)} custom-call(f32[3,4,4,4,8,256]{5,4,3,2,1,0:T(8,128)S(1)} %get-tuple-element.25.w, f32[4,4,4,8,128]{4,3,2,1,0:T(8,128)S(1)} %get-tuple-element.26.strip, f32[8,256]{1,0:T(8,128)S(1)} %copy-done, f32[8,256]{1,0:T(8,128)S(1)} %copy-done.1, f32[8,128]{1,0:T(8,128)S(1)} %get-tuple-element.23.strip_v, ...), custom_call_target="tpu_custom_call" | custom-call | flops 11796480 | bytes 3145728 | tf_op jit(solution)/shard_map/edge/pallas_call | solution.py:782
Async XLA Ops:
  0.6 34.8 %copy-start.1 = (f32[8,256]{1,0:T(8,128)S(1)}, f32[8,256]{1,0:T(8,128)}, u32[]{:S(2)}) copy-start(f32[8,256]{1,0:T(8,128)} %speed.7) | copy-start | bytes 24580
  0.6 34.8 %copy-start = (f32[8,256]{1,0:T(8,128)S(1)}, f32[8,256]{1,0:T(8,128)}, u32[]{:S(2)}) copy-start(f32[8,256]{1,0:T(8,128)} %visc.7) | copy-start | bytes 24580
  30.8 8.6 %collective-permute-start = (f32[9,8,128]{2,1,0:T(8,128)S(1)}, f32[9,8,128]{2,1,0:T(8,128)S(1)}, u32[]{:S(2)}, u32[]{:S(2)}) collective-permute-start(f32[9,8,128]{2,1,0:T(8,128)S(1)} %get-tuple-element.18), channel_id=1, source_target_pairs={{0,8},{8,0},{16,24},{24,16},{1,9},{9,1},{17,25},{25,17},{2,10},{10... | collective-permute-start | bytes 110600 | tf_op jit(solution)/shard_map/ppermute | solution.py:710
  30.9 8.5 %collective-permute-start.1 = (f32[9,8,128]{2,1,0:T(8,128)S(1)}, f32[9,8,128]{2,1,0:T(8,128)S(1)}, u32[]{:S(2)}, u32[]{:S(2)}) collective-permute-start(f32[9,8,128]{2,1,0:T(8,128)S(1)} %get-tuple-element.19), channel_id=1, source_target_pairs={{8,16},{16,8},{9,17},{17,9},{10,18},{18,10},{11,19},{19,11},{12,20... | collective-permute-start | bytes 110600 | tf_op jit(solution)/shard_map/ppermute | solution.py:710
  40.7 10.1 %collective-permute-start.2 = (f32[29,8,256]{2,1,0:T(8,128)S(1)}, f32[29,8,256]{2,1,0:T(8,128)S(1)}, u32[]{:S(2)}, u32[]{:S(2)}) collective-permute-start(f32[29,8,256]{2,1,0:T(8,128)S(1)} %get-tuple-element.27.sent_first), channel_id=1, source_target_pairs={{0,1},{1,0},{2,3},{3,2},{4,5},{5,4},{6,7},{7,6},{8,9},{9,8},{10,11... | collective-permute-start | bytes 712712 | tf_op jit(solution)/shard_map/ppermute | solution.py:710
  42.0 8.8 %collective-permute-start.3 = (f32[29,8,256]{2,1,0:T(8,128)S(1)}, f32[29,8,256]{2,1,0:T(8,128)S(1)}, u32[]{:S(2)}, u32[]{:S(2)}) collective-permute-start(f32[29,8,256]{2,1,0:T(8,128)S(1)} %get-tuple-element.28.sent_second), channel_id=1, source_target_pairs={{1,2},{2,1},{3,4},{4,3},{5,6},{6,5},{9,10},{10,9},{11,12},{12,11},... | collective-permute-start | bytes 712712 | tf_op jit(solution)/shard_map/ppermute | solution.py:710

commit v4 on v3

--- a/solution.py
+++ b/solution.py
@@ -375,6 +375,7 @@
     z_two,
     e_visc,
     e_speed,
+    sent,
 ):
     cells = w.shape[-1]
     tiles = cells // LANE
@@ -501,10 +502,13 @@
                     value = jnp.where(
                         lane >= LANE - 4, pltpu.roll(edge, LANE - 4 - 68 - 16 * comp, 1), value
                     )
-                out[comp, a, b, c, :, at] = value
+                e_one[comp, a, b, c, :, at] = value
+        pltpu.make_async_copy(e_one.at[comp], out.at[comp], sent.at[comp]).start()
         return carry
 
     lax.fori_loop(0, 3, finish, 0)
+    for comp in range(3):
+        pltpu.make_async_copy(e_one.at[comp], out.at[comp], sent.at[comp]).wait()
 
 
 def particle_kernel(
@@ -557,6 +561,12 @@
     ]
     for copy in copies:
         copy.start()
+    sums = (sums_even, sums_odd)
+    for buffer in sums:
+        buffer[...] = jnp.zeros(buffer.shape, f32)
+    totals[...] = jnp.zeros(totals.shape, f32)
+    one_hot[...] = jnp.zeros(one_hot.shape, bf16)
+    rows_ref[...] = jnp.full(rows_ref.shape, -1.0, f32)
     bins = positions.shape[1]
     groups = bins // SUB
     lanes_bins = one_hot.shape[0]
@@ -568,7 +578,6 @@
     copies[0].wait()
     copies[1].wait()
 
-    rows_ref[...] = jnp.full(rows_ref.shape, -1.0, f32)
     rows_ref[0:1, :bins] = element_row[...].astype(f32)
     rows_ref[1:2, :bins] = fill_row[...].astype(f32)
     element_lanes = rows_ref[0:1, :]
@@ -578,7 +587,6 @@
 
     lane_bins = iota((SUB, lanes_bins), 1)
     row_bins = iota((SUB, lanes_bins), 0)
-    one_hot[...] = jnp.zeros(one_hot.shape, bf16)
     for g in range(groups):
         own = lane_bins == row_bins + g * SUB
         element = jnp.sum(jnp.where(own, element_lanes, 0.0), axis=1, keepdims=True)
@@ -620,9 +628,6 @@
     for copy in copies[3:]:
         copy.wait()
     rates[...] = relax[...] * occupied[...]
-    totals[...] = jnp.zeros(totals.shape, f32)
-
-    sums = (sums_even, sums_odd)
 
     def sum_lanes(first, turn):
         buffer = sums[first // GROUPS_TOGETHER % 2]
@@ -674,8 +679,6 @@
                     buffer[slot, j] = buffer[slot, j] + square * weighs[a]
         return carry
 
-    for buffer in sums:
-        buffer[...] = jnp.zeros(buffer.shape, f32)
     for first in range(0, groups, GROUPS_TOGETHER):
         lax.fori_loop(0, SUBSTEPS, functools.partial(substep, first), 0)
     for turn in range(16):
@@ -778,13 +781,13 @@
         )
     )
 
-    def call(kernel, name, outputs, scratch, *operands):
+    def call(kernel, name, outputs, scratch, *operands, place=None, more=()):
         return pl.pallas_call(
             kernel,
             out_shape=outputs,
             in_specs=[vmem] * len(operands),
-            out_specs=jax.tree.map(lambda _: vmem, outputs),
-            scratch_shapes=[pltpu.VMEM(shape.shape, f32) for shape in scratch],
+            out_specs=jax.tree.map(lambda _: place or vmem, outputs),
+            scratch_shapes=[pltpu.VMEM(shape.shape, f32) for shape in scratch] + list(more),
             compiler_params=params,
             cost_estimate=pl.CostEstimate(
                 flops=30 * fluid_velocity.size, bytes_accessed=8 * fluid_velocity.size, transcendentals=0
@@ -834,6 +837,8 @@
         strip_g,
         *sent,
         *got,
+        place=hbm,
+        more=(pltpu.SemaphoreType.DMA((3,)),),
     )
     return (q.reshape(3, NODES, sec_cells, air_cells), particles_out.transpose(1, 0, 2))
 

time: 57.8 us -> 56.9 us (0.984)
  Pallas kernels: 43.7 us -> 42.6 us
    pallas_call x1, Pallas kernels: 30.2 us -> 29.4 us  [local(): pl.pallas_call(particle_kernel, out_shape=(field, jax.ShapeDtypeStruct((6...]
  transfers between devices with their start and end apart: 4 -> 4, of which waited for: 1 -> 1; matrix products, arithmetic and copies ran while one was open for 0% -> 0% of each run, Pallas kernels for 9% -> 10%
where the time goes in v4:
time: 56.9 us; the launch traced here: 56.7 us
  Pallas kernels  42.6 us (75%)
  starting transfers between devices  6.72 us (12%)
  waiting for transfers between devices  6.46 us (11%)
  between operations  0.88 us (2%)
    pallas_call x1, Pallas kernels, local(): pl.pallas_call(particle_kernel, out_shape=(field, jax.ShapeDtypeStruct((6...  29.4 us
    pallas_call x4, Pallas kernels, call(): pl.pallas_call(kernel, out_shape=outputs, in_specs=[vmem] * len(operands)...  13.2 us
    ppermute x4, starting transfers between devices, swap(): return lax.ppermute(values, axis, pairs)  6.72 us
    ppermute x4, waiting for transfers between devices, swap(): return lax.ppermute(values, axis, pairs)  6.46 us
  transfers between devices with their start and end apart: 4, of which 1 were waited for; matrix products, arithmetic and copies ran while one was open for 0% of the time, Pallas kernels for 10%

profile of v4, /device:TPU:1, one launch (start us, length us, event | category | flops | bytes accessed | tf_op | source)
XLA Modules:
  0.0 56.7 jit_solution(12081170195040135591)
XLA Ops:
  0.6 0.0 copy-start.1
  0.6 0.0 copy-start
  0.7 29.4 %particles.1 = (f32[3,4,4,4,8,256]{5,4,3,2,1,0:T(8,128)S(1)}, f32[6,96,128]{2,1,0:T(8,128)}, f32[9,8,128]{2,1,0:T(8,128)S(1)}, f32[9,8,128]{2,1,0:T(8,128)S(1)}) custom-call(f32[3,4,4,4,8,256]{5,4,3,2,1,0:T(8,128)} %bitcast.7, f32[8,256]{1,0:T(8,128)} %mass_hbm.1, f32[3,96,128]{2,1,0:T(8,128)} %bitcast.9, f32[3,96,128]{2,1,0:T(8,128)} %bitcast.10, ...), custom_call_target="tpu_custom_call" | custom-call | tf_op jit(solution)/shard_map/particles/pallas_call | solution.py:741
  30.0 0.1 collective-permute-start
  30.1 4.5 %collective-permute-start.1 = (f32[9,8,128]{2,1,0:T(8,128)S(1)}, f32[9,8,128]{2,1,0:T(8,128)S(1)}, u32[]{:S(2)}, u32[]{:S(2)}) collective-permute-start(f32[9,8,128]{2,1,0:T(8,128)S(1)} %get-tuple-element.19), channel_id=1, source_target_pairs={{8,16},{16,8},{9,17},{17,9},{10,18},{18,10},{11,19},{19,11},{12,20... | collective-permute-start | bytes 110600 | tf_op jit(solution)/shard_map/ppermute | solution.py:713
  34.6 0.0 copy-done.1
  34.6 0.0 copy-done
  34.7 3.9 %main.1 = (f32[3,4,4,4,8,256]{5,4,3,2,1,0:T(8,128)S(1)}, f32[24,8,256]{2,1,0:T(8,128)S(1)}, f32[24,8,256]{2,1,0:T(8,128)S(1)}) custom-call(f32[3,4,4,4,8,256]{5,4,3,2,1,0:T(8,128)S(1)} %get-tuple-element.16.q, f32[8,256]{1,0:T(8,128)S(1)} %copy-done, f32[8,256]{1,0:T(8,128)S(1)} %copy-done.1), custom_call_target="tpu_custom_call" | custom-call | flops 11796480 | bytes 3145728 | tf_op jit(solution)/shard_map/main/pallas_call | solution.py:785
  38.6 0.0 collective-permute-done.air_first
  38.6 0.0 collective-permute-done.1.air_second
  38.6 1.3 %strip.1 = (f32[4,4,4,8,128]{4,3,2,1,0:T(8,128)S(1)}, f32[8,128]{1,0:T(8,128)S(1)}, f32[8,128]{1,0:T(8,128)S(1)}, f32[29,8,256]{2,1,0:T(8,128)S(1)}, f32[29,8,256]{2,1,0:T(8,128)S(1)}) custom-call(f32[3,4,4,4,8,256]{5,4,3,2,1,0:T(8,128)S(1)} %get-tuple-element.16.q, f32[8,256]{1,0:T(8,128)S(1)} %copy-done, f32[8,256]{1,0:T(8,128)S(1)} %copy-done.1, ...), custom_call_target="tpu_custom_call" | custom-call | flops 11796480 | bytes 3145728 | tf_op jit(solution)/shard_map/strip/pallas_call | solution.py:785
  39.9 1.3 %collective-permute-start.2 = (f32[29,8,256]{2,1,0:T(8,128)S(1)}, f32[29,8,256]{2,1,0:T(8,128)S(1)}, u32[]{:S(2)}, u32[]{:S(2)}) collective-permute-start(f32[29,8,256]{2,1,0:T(8,128)S(1)} %get-tuple-element.27.sent_first), channel_id=1, source_target_pairs={{0,1},{1,0},{2,3},{3,2},{4,5},{5,4},{6,7},{7,6},{8,9},{9,8},{10,11... | collective-permute-start | bytes 712712 | tf_op jit(solution)/shard_map/ppermute | solution.py:713
  41.2 0.8 %collective-permute-start.3 = (f32[29,8,256]{2,1,0:T(8,128)S(1)}, f32[29,8,256]{2,1,0:T(8,128)S(1)}, u32[]{:S(2)}, u32[]{:S(2)}) collective-permute-start(f32[29,8,256]{2,1,0:T(8,128)S(1)} %get-tuple-element.28.sent_second), channel_id=1, source_target_pairs={{1,2},{2,1},{3,4},{4,3},{5,6},{6,5},{9,10},{10,9},{11,12},{12,11},... | collective-permute-start | bytes 712712 | tf_op jit(solution)/shard_map/ppermute | solution.py:713
  42.0 1.5 %fourth.1 = (f32[3,4,4,4,8,256]{5,4,3,2,1,0:T(8,128)S(1)}, f32[4,4,4,8,128]{4,3,2,1,0:T(8,128)S(1)}) custom-call(f32[3,4,4,4,8,256]{5,4,3,2,1,0:T(8,128)S(1)} %get-tuple-element.17.w, f32[4,4,4,8,128]{4,3,2,1,0:T(8,128)S(1)} %get-tuple-element.22.strip, f32[8,256]{1,0:T(8,128)S(1)} %copy-done, f32[8,256]{1,0:T(8,128)S(1)} %copy-done.1, ...), custom_call_target="tpu_custom_call" | custom-call | flops 11796480 | bytes 3145728 | tf_op jit(solution)/shard_map/fourth/pallas_call | solution.py:785
  43.5 6.5 %collective-permute-done.2.got_first = f32[29,8,256]{2,1,0:T(8,128)S(1)} collective-permute-done((f32[29,8,256]{2,1,0:T(8,128)S(1)}, f32[29,8,256]{2,1,0:T(8,128)S(1)}, u32[]{:S(2)}, u32[]{:S(2)}) %collective-permute-start.2) | collective-permute-done | bytes 237600 | tf_op jit(solution)/shard_map/ppermute | solution.py:713
  50.0 0.0 collective-permute-done.3.got_second
  50.0 6.6 %edge.1 = f32[3,4,4,4,8,256]{5,4,3,2,1,0:T(8,128)} custom-call(f32[3,4,4,4,8,256]{5,4,3,2,1,0:T(8,128)S(1)} %get-tuple-element.25.w, f32[4,4,4,8,128]{4,3,2,1,0:T(8,128)S(1)} %get-tuple-element.26.strip, f32[8,256]{1,0:T(8,128)S(1)} %copy-done, f32[8,256]{1,0:T(8,128)S(1)} %copy-done.1, f32[8,128]{1,0:T(8,128)S(1)} %get-tuple-element.23.strip_v, ...), custom_call_target="tpu_custom_call" | custom-call | flops 11796480 | bytes 3145728 | tf_op jit(solution)/shard_map/edge/pallas_call | solution.py:785
Async XLA Ops:
  0.6 34.0 %copy-start.1 = (f32[8,256]{1,0:T(8,128)S(1)}, f32[8,256]{1,0:T(8,128)}, u32[]{:S(2)}) copy-start(f32[8,256]{1,0:T(8,128)} %speed.7) | copy-start | bytes 24580
  0.6 34.0 %copy-start = (f32[8,256]{1,0:T(8,128)S(1)}, f32[8,256]{1,0:T(8,128)}, u32[]{:S(2)}) copy-start(f32[8,256]{1,0:T(8,128)} %visc.7) | copy-start | bytes 24580
  30.0 8.6 %collective-permute-start = (f32[9,8,128]{2,1,0:T(8,128)S(1)}, f32[9,8,128]{2,1,0:T(8,128)S(1)}, u32[]{:S(2)}, u32[]{:S(2)}) collective-permute-start(f32[9,8,128]{2,1,0:T(8,128)S(1)} %get-tuple-element.18), channel_id=1, source_target_pairs={{0,8},{8,0},{16,24},{24,16},{1,9},{9,1},{17,25},{25,17},{2,10},{10... | collective-permute-start | bytes 110600 | tf_op jit(solution)/shard_map/ppermute | solution.py:713
  30.1 8.5 %collective-permute-start.1 = (f32[9,8,128]{2,1,0:T(8,128)S(1)}, f32[9,8,128]{2,1,0:T(8,128)S(1)}, u32[]{:S(2)}, u32[]{:S(2)}) collective-permute-start(f32[9,8,128]{2,1,0:T(8,128)S(1)} %get-tuple-element.19), channel_id=1, source_target_pairs={{8,16},{16,8},{9,17},{17,9},{10,18},{18,10},{11,19},{19,11},{12,20... | collective-permute-start | bytes 110600 | tf_op jit(solution)/shard_map/ppermute | solution.py:713
  39.9 10.1 %collective-permute-start.2 = (f32[29,8,256]{2,1,0:T(8,128)S(1)}, f32[29,8,256]{2,1,0:T(8,128)S(1)}, u32[]{:S(2)}, u32[]{:S(2)}) collective-permute-start(f32[29,8,256]{2,1,0:T(8,128)S(1)} %get-tuple-element.27.sent_first), channel_id=1, source_target_pairs={{0,1},{1,0},{2,3},{3,2},{4,5},{5,4},{6,7},{7,6},{8,9},{9,8},{10,11... | collective-permute-start | bytes 712712 | tf_op jit(solution)/shard_map/ppermute | solution.py:713
  41.2 8.8 %collective-permute-start.3 = (f32[29,8,256]{2,1,0:T(8,128)S(1)}, f32[29,8,256]{2,1,0:T(8,128)S(1)}, u32[]{:S(2)}, u32[]{:S(2)}) collective-permute-start(f32[29,8,256]{2,1,0:T(8,128)S(1)} %get-tuple-element.28.sent_second), channel_id=1, source_target_pairs={{1,2},{2,1},{3,4},{4,3},{5,6},{6,5},{9,10},{10,9},{11,12},{12,11},... | collective-permute-start | bytes 712712 | tf_op jit(solution)/shard_map/ppermute | solution.py:713
